TPU v7x, 128 devices: a whole 4x4x4 slice. The times are simulated.
128 devices in a mesh: cfg: 2 (over core), req: 4 (over y), seq: 16 (over z, x).
Axes of the slice: x: 4, y: 4, z: 4, core: 2. Of those that a mesh axis runs over, the one named last changes fastest.
Arguments:
- latent: float32 [8, 2048, 64], P('req', 'seq'), may hold values from -6 to 6
- hidden_in: bfloat16 [2, 8, 2048, 2432], P('cfg', 'req', 'seq'), may hold values from -25 to 25
- img_query: bfloat16 [2, 8, 2048, 2432], P('cfg', 'req', 'seq'), may hold values from -10 to 10
- img_key: bfloat16 [2, 8, 2048, 2432], P('cfg', 'req', 'seq'), may hold values from -10 to 10
- img_value: bfloat16 [2, 8, 2048, 2432], P('cfg', 'req', 'seq'), may hold values from -6 to 6
- txt_key: bfloat16 [2, 8, 160, 2432], P('cfg', 'req', 'seq'), may hold values from -10 to 10
- txt_value: bfloat16 [2, 8, 160, 2432], P('cfg', 'req', 'seq'), may hold values from -6 to 6
- text_len: int32 [2, 8], P('cfg', 'req'), may hold values from 38 to 154, as said below
- head_slot: int32 [38], replicated, may hold values from 0 to 47, as said below
- out_weight: bfloat16 [2432, 2432], replicated, may hold values from -0.125 to 0.125
- out_bias: float32 [2432], replicated, may hold values from -3 to 3
- attn_gate: float32 [2, 8, 2432], P('cfg', 'req'), may hold values from 0.5 to 2
- final_mod: float32 [2, 8, 2, 2432], P('cfg', 'req'), may hold values from -3 to 3
- final_weight: bfloat16 [2432, 64], replicated, may hold values from -0.125 to 0.125
- final_bias: float32 [64], replicated, may hold values from -3 to 3
- timesteps: int32 [8], P('req'), may hold values from 1 to 28
- guidance: float32 [8], P('req'), may hold values from 2.5 to 6
Outputs:
- velocity: float32 [8, 2048, 64], P('req', 'seq')
- latent_next: float32 [8, 2048, 64], P('req', 'seq')
- hidden_norms: float32 [2, 8], P('cfg', 'req')
- max_logits: float32 [48], P('seq')
Inputs may be any that keep to these rules, and one draw needn't show every extreme that they name: `head_slot`: distinct heads take distinct slots; slots j * 3 to (j + 1) * 3 - 1 belong to index j of seq, and every index holds 3 heads or one fewer. Text positions below text_len are live; some half and request has exactly 154 live text tokens.
All inputs are finite; a program needn't handle non-finite values.
Results may differ from a plain program's by a relative error of at most 0.0032.
Values may be sent and summed in bfloat16 or wider, within the bound.
No kernel may reach another device: no remote copies, remote signals or barrier semaphores. Data moves between devices by JAX's collectives and lax.ppermute only.
A program may use at most 128 MiB of HBM per device.

v0:
```python
import math

import jax
import jax.numpy as jnp
from jax import lax
from jax.sharding import PartitionSpec as P

STEPS = 28


masked_score = -1e30


def sigma_of(step_idx):
    fraction = step_idx.astype(jnp.float32) / STEPS
    return 3.0 * fraction / (1.0 + 2.0 * fraction)


def attend(query_rows, all_keys, all_values, length):
    row_count = query_rows.shape[0]
    head_dim = query_rows.shape[1]
    block_rows = min(512, row_count)
    key_valid = jnp.arange(all_keys.shape[0], dtype=jnp.int32) < row_count + length

    def one_block(query_block):
        scores = jnp.einsum(
            "qd,kd->qk", query_block, all_keys, preferred_element_type=jnp.float32
        ) * (1.0 / math.sqrt(head_dim))
        scores = jnp.where(key_valid[None, :], scores, masked_score)
        row_top = jnp.max(scores, axis=1, keepdims=True)
        weights = jnp.exp(scores - row_top)
        weights = (weights / jnp.sum(weights, axis=1, keepdims=True)).astype(jnp.bfloat16)
        result = jnp.dot(weights, all_values, preferred_element_type=jnp.float32).astype(
            jnp.bfloat16
        )
        return (result, jnp.max(row_top))

    outputs, block_tops = lax.map(
        one_block, query_rows.reshape(row_count // block_rows, block_rows, head_dim)
    )
    return (outputs.reshape(row_count, head_dim), jnp.max(block_tops))


def run_item(packed):
    return attend(packed[0], packed[1], packed[2], packed[3])


def local(
    latent,
    hidden_in,
    img_query,
    img_key,
    img_value,
    txt_key,
    txt_value,
    text_len,
    head_slot,
    out_weight,
    out_bias,
    attn_gate,
    final_mod,
    final_weight,
    final_bias,
    timesteps,
    guidance,
):
    shards = lax.axis_size("seq")
    position = lax.axis_index("seq")
    head_count = head_slot.shape[0]
    model_width = out_weight.shape[0]
    head_dim = model_width // head_count
    groups = img_query.shape[1]
    tok_local = img_query.shape[2]
    image_rows = tok_local * shards
    per_shard = (head_count + shards - 1) // shards
    slot_count = per_shard * shards
    lengths = text_len[0]
    slot_ids = jnp.arange(slot_count, dtype=jnp.int32)
    slot_match = head_slot[None, :] == slot_ids[:, None]
    slot_used = jnp.any(slot_match, axis=1)
    own_used = lax.dynamic_slice_in_dim(slot_used, position * per_shard, per_shard)
    head_ids = jnp.arange(head_count, dtype=jnp.int32)
    streams = (img_query[0], img_key[0], img_value[0], txt_key[0], txt_value[0])
    slot_head = jnp.sum(jnp.where(slot_match, head_ids[None, :], 0), axis=1) + jnp.where(
        slot_used, 0, head_count
    )

    def to_slots(tensor):
        row_count = tensor.shape[1]
        split_heads = tensor.reshape(groups, row_count, head_count, head_dim)
        padded = jnp.concatenate(
            [split_heads, jnp.zeros((groups, row_count, 1, head_dim), tensor.dtype)], axis=2
        )
        return jnp.take(padded, slot_head, axis=2).reshape(
            groups, row_count, shards, per_shard * head_dim
        )

    received = (
        lax.all_to_all(to_slots(streams[0]), "seq", split_axis=2, concat_axis=1, tiled=True),
        lax.all_to_all(to_slots(streams[1]), "seq", split_axis=2, concat_axis=1, tiled=True),
        lax.all_to_all(to_slots(streams[2]), "seq", split_axis=2, concat_axis=1, tiled=True),
        lax.all_to_all(to_slots(streams[3]), "seq", split_axis=2, concat_axis=1, tiled=True),
        lax.all_to_all(to_slots(streams[4]), "seq", split_axis=2, concat_axis=1, tiled=True),
    )

    def by_slot(tensor):
        row_count = tensor.shape[1]
        return (
            tensor.reshape(groups, row_count, per_shard, head_dim)
            .transpose(0, 2, 1, 3)
            .reshape(groups * per_shard, row_count, head_dim)
        )

    queries = by_slot(received[0])
    all_keys = jnp.concatenate([by_slot(received[1]), by_slot(received[3])], axis=1)
    all_values = jnp.concatenate([by_slot(received[2]), by_slot(received[4])], axis=1)
    item_lengths = jnp.repeat(lengths, per_shard)
    outputs, top_scores = lax.map(run_item, (queries, all_keys, all_values, item_lengths))
    outgoing = (
        outputs.reshape(groups, per_shard, image_rows, head_dim)
        .transpose(0, 2, 1, 3)
        .reshape(groups, image_rows, 1, per_shard * head_dim)
    )
    returned = lax.all_to_all(outgoing, "seq", split_axis=1, concat_axis=2, tiled=True)
    attended = jnp.take(
        returned.reshape(groups, tok_local, slot_count, head_dim), head_slot, axis=2
    ).reshape(groups, tok_local, model_width)
    slot_top = lax.pmax(jnp.max(top_scores.reshape(groups, per_shard), axis=0), ("cfg", "req"))
    max_logits = jnp.where(own_used, slot_top, 0.0)
    projected = (
        jnp.dot(
            attended.reshape(groups * tok_local, model_width),
            out_weight,
            preferred_element_type=jnp.float32,
        )
        + out_bias
    )
    hidden = hidden_in[0].astype(jnp.float32) + attn_gate[0][:, None, :] * projected.reshape(
        groups, tok_local, model_width
    )
    square_sums = lax.psum(jnp.sum(hidden * hidden, axis=(1, 2)), "seq")
    hidden_norms = jnp.sqrt(square_sums / (image_rows * model_width))[None, :]
    row_mean = jnp.mean(hidden, axis=2, keepdims=True)
    centered = hidden - row_mean
    row_var = jnp.mean(centered * centered, axis=2, keepdims=True)
    modul = final_mod[0]
    normed = (
        centered / jnp.sqrt(row_var + 1e-06) * (1.0 + modul[:, 1][:, None, :])
        + modul[:, 0][:, None, :]
    ).astype(jnp.bfloat16)
    prediction = (
        jnp.dot(
            normed.reshape(groups * tok_local, model_width),
            final_weight,
            preferred_element_type=jnp.float32,
        )
        + final_bias
    )
    prediction = prediction.reshape(groups, tok_local, final_weight.shape[1])
    half_weight = jnp.where(lax.axis_index("cfg") == 0, guidance, 1.0 - guidance)
    velocity = lax.psum(half_weight[:, None, None] * prediction, "cfg")
    step_size = (sigma_of(timesteps - 1) - sigma_of(timesteps))[:, None, None]
    latent_next = latent + step_size * velocity
    return (velocity, latent_next, hidden_norms, max_logits)


def solution(mesh):
    in_specs = (
        P("req", "seq", None),
        P("cfg", "req", "seq", None),
        P("cfg", "req", "seq", None),
        P("cfg", "req", "seq", None),
        P("cfg", "req", "seq", None),
        P("cfg", "req", "seq", None),
        P("cfg", "req", "seq", None),
        P("cfg", "req"),
        P(),
        P(),
        P(),
        P("cfg", "req", None),
        P("cfg", "req", None, None),
        P(),
        P(),
        P("req"),
        P("req"),
    )
    out_specs = (P("req", "seq", None), P("req", "seq", None), P("cfg", "req"), P("seq"))
    return jax.shard_map(local, mesh=mesh, in_specs=in_specs, out_specs=out_specs, check_vma=False)
```

profile of v0, /device:TPU:0, one launch (start us, length us, event | category | flops | bytes accessed | tf_op | source)
XLA Modules:
  0.0 396.5 jit_solution(15232788555272955208)
XLA Ops:
  16.1 8.0 %all-to-all-start.2 = ((bf16[2,10,16,192]{3,0,1,2:T(2,128)(2,1)}), bf16[2,10,16,192]{3,0,1,2:T(2,128)(2,1)}, u32[]{:S(2)}, u32[]{:S(2)}) async-start(bf16[2,10,16,192]{3,0,1,2:T(2,128)(2,1)} %copy.148), calls=%async_computation.2 | async-start | bytes 327680 | tf_op jit(solution)/shard_map/all_to_all | solution.py:102
  38.5 7.2 %all-to-all-start.4 = ((bf16[2,10,16,192]{3,0,1,2:T(2,128)(2,1)}), bf16[2,10,16,192]{3,0,1,2:T(2,128)(2,1)}, u32[]{:S(2)}, u32[]{:S(2)}) async-start(bf16[2,10,16,192]{3,0,1,2:T(2,128)(2,1)} %copy.158), calls=%async_computation.4 | async-start | bytes 327680 | tf_op jit(solution)/shard_map/all_to_all | solution.py:103
  53.9 3.9 all-to-all-start.1
  59.2 21.0 %all-to-all-done.1 = bf16[2,128,16,192]{1,3,0,2:T(8,128)(2,1)S(1)} async-done(((bf16[2,128,16,192]{1,3,0,2:T(8,128)(2,1)}), bf16[2,128,16,192]{1,3,0,2:T(8,128)(2,1)S(1)}, u32[]{:S(2)}, u32[]{:S(2)}) %all-to-all-start.1) | async-done | bytes 1572896 | tf_op jit(solution)/shard_map/all_to_all | solution.py:100
  80.2 3.7 all-to-all-start.3
  86.8 19.4 %all-to-all-done.3 = bf16[2,128,16,192]{1,3,0,2:T(8,128)(2,1)S(1)} async-done(((bf16[2,128,16,192]{1,3,0,2:T(8,128)(2,1)}), bf16[2,128,16,192]{1,3,0,2:T(8,128)(2,1)S(1)}, u32[]{:S(2)}, u32[]{:S(2)}) %all-to-all-start.3) | async-done | bytes 1572896 | tf_op jit(solution)/shard_map/all_to_all | solution.py:101
  106.1 4.6 %all-to-all-start = ((bf16[2,128,16,192]{1,3,0,2:T(8,128)(2,1)}), bf16[2,128,16,192]{1,3,0,2:T(8,128)(2,1)}, u32[]{:S(2)}, u32[]{:S(2)}) async-start(bf16[2,128,16,192]{1,3,0,2:T(8,128)(2,1)} %copy.140), calls=%async_computation | async-start | bytes 3145728 | tf_op jit(solution)/shard_map/all_to_all | solution.py:99
  130.3 3.7 reshape.159
  134.0 4.1 %copy.160 = bf16[6,2048,64]{2,1,0:T(8,128)(2,1)} copy(bf16[6,2048,64]{1,2,0:T(8,128)(2,1)} %bitcast.192) | data formatting | bytes 3145728 | tf_op jit(solution)/shard_map/reshape | solution.py:111
  141.7 3.7 reshape.149
  145.4 5.0 %pad_maximum_fusion = (bf16[6,2208,64]{2,1,0:T(8,128)(2,1)}, bf16[6,2208,64]{2,1,0:T(8,128)(2,1)}) fusion(bf16[6,160,64]{2,1,0:T(8,128)(2,1)} %bitcast.200, bf16[6,2048,64]{2,1,0:T(8,128)(2,1)S(1)} %copy.150, bf16[6,160,64]{2,1,0:T(8,128)(2,1)} %bitcast.201, bf16[6,2048,64]{2,1,0:T(8,128)(2,1)} %copy.160), kind=kLoop, calls=%fused_computation.25 | loop fusion | flops 6782976 | bytes 6782976 | tf_op jit(solution)/shard_map/concatenate | solution.py:115
  150.4 139.8 %while.26 = (s32[]{:T(128)}, bf16[6,2048,64]{1,2,0:T(8,128)(2,1)}, f32[6]{0:T(128)S(1)}, bf16[6,2048,64]{1,2,0:T(8,128)(2,1)}, bf16[6,2208,64]{2,1,0:T(8,128)(2,...) while((s32[]{:T(128)}, bf16[6,2048,64]{1,2,0:T(8,128)(2,1)}, ...), condition=%wide.region_9.12_spmd, body=%wide.region_2.11_spmd.sunk | while | flops 299615392 | bytes 18661392 | solution.py:118
  154.1 17.0 %while.27 = (s32[]{:T(128)}, bf16[4,512,64]{1,2,0:T(8,128)(2,1)S(1)}, f32[4]{0:T(128)S(1)}, bf16[4,512,64]{2,1,0:T(8,128)(2,1)S(1)}, bf16[2208,64]{1,0:T(8,128)(...) while((s32[]{:T(128)}, bf16[4,512,64]{1,2,0:T(8,128)(2,1)S(1)}, ...), condition=%wide.region_7.9_spmd.clone, body=%wide.region_3.0_spmd.clone.sunk | while | flops 299615392 | bytes 14908689 | solution.py:38
  177.4 17.0 %while.27 = (s32[]{:T(128)}, bf16[4,512,64]{1,2,0:T(8,128)(2,1)S(1)}, f32[4]{0:T(128)S(1)}, bf16[4,512,64]{2,1,0:T(8,128)(2,1)S(1)}, bf16[2208,64]{1,0:T(8,128)(...) while((s32[]{:T(128)}, bf16[4,512,64]{1,2,0:T(8,128)(2,1)S(1)}, ...), condition=%wide.region_7.9_spmd.clone, body=%wide.region_3.0_spmd.clone.sunk | while | flops 299615392 | bytes 14908689 | solution.py:38
  200.7 17.0 %while.27 = (s32[]{:T(128)}, bf16[4,512,64]{1,2,0:T(8,128)(2,1)S(1)}, f32[4]{0:T(128)S(1)}, bf16[4,512,64]{2,1,0:T(8,128)(2,1)S(1)}, bf16[2208,64]{1,0:T(8,128)(...) while((s32[]{:T(128)}, bf16[4,512,64]{1,2,0:T(8,128)(2,1)S(1)}, ...), condition=%wide.region_7.9_spmd.clone, body=%wide.region_3.0_spmd.clone.sunk | while | flops 299615392 | bytes 14908689 | solution.py:38
  223.9 17.0 %while.27 = (s32[]{:T(128)}, bf16[4,512,64]{1,2,0:T(8,128)(2,1)S(1)}, f32[4]{0:T(128)S(1)}, bf16[4,512,64]{2,1,0:T(8,128)(2,1)S(1)}, bf16[2208,64]{1,0:T(8,128)(...) while((s32[]{:T(128)}, bf16[4,512,64]{1,2,0:T(8,128)(2,1)S(1)}, ...), condition=%wide.region_7.9_spmd.clone, body=%wide.region_3.0_spmd.clone.sunk | while | flops 299615392 | bytes 14908689 | solution.py:38
  247.2 17.0 %while.27 = (s32[]{:T(128)}, bf16[4,512,64]{1,2,0:T(8,128)(2,1)S(1)}, f32[4]{0:T(128)S(1)}, bf16[4,512,64]{2,1,0:T(8,128)(2,1)S(1)}, bf16[2208,64]{1,0:T(8,128)(...) while((s32[]{:T(128)}, bf16[4,512,64]{1,2,0:T(8,128)(2,1)S(1)}, ...), condition=%wide.region_7.9_spmd.clone, body=%wide.region_3.0_spmd.clone.sunk | while | flops 299615392 | bytes 14908689 | solution.py:38
  270.5 17.0 %while.27 = (s32[]{:T(128)}, bf16[4,512,64]{1,2,0:T(8,128)(2,1)S(1)}, f32[4]{0:T(128)S(1)}, bf16[4,512,64]{2,1,0:T(8,128)(2,1)S(1)}, bf16[2208,64]{1,0:T(8,128)(...) while((s32[]{:T(128)}, bf16[4,512,64]{1,2,0:T(8,128)(2,1)S(1)}, ...), condition=%wide.region_7.9_spmd.clone, body=%wide.region_3.0_spmd.clone.sunk | while | flops 299615392 | bytes 14908689 | solution.py:38
  290.1 6.0 %copy.164 = bf16[2,2048,1,192]{3,0,2,1:T(2,128)(2,1)} copy(bf16[2,2048,1,192]{1,3,0,2:T(8,128)(2,1)} %bitcast.197) | data formatting | bytes 3145728 | tf_op jit(solution)/shard_map/reshape | solution.py:122
  296.2 7.0 %all-to-all-start.5 = ((bf16[2,2048,1,192]{3,0,2,1:T(2,128)(2,1)}), bf16[2,2048,1,192]{3,0,2,1:T(2,128)(2,1)S(1)}, u32[]{:S(2)}, u32[]{:S(2)}) async-start(bf16[2,2048,1,192]{3,0,2,1:T(2,128)(2,1)} %copy.164), calls=%async_computation.5 | async-start | bytes 4194304 | tf_op jit(solution)/shard_map/all_to_all | solution.py:124
  303.5 15.0 %pmax.7 = f32[3]{0:T(128)S(1)} all-reduce(f32[3]{0:T(128)S(1)} %reduce_max.36), channel_id=1, replica_groups=mesh['cfg'=2,'req'=4,'seq'=16] {'cfg','req'}, use_global_device_ids=true, to_apply=%region_16.19 | all-reduce | flops 3 | bytes 24 | tf_op jit(solution)/shard_map/pmax | solution.py:128
  319.1 11.6 %all-to-all-done.5 = bf16[2,2048,1,192]{3,0,2,1:T(2,128)(2,1)S(1)} async-done(((bf16[2,2048,1,192]{3,0,2,1:T(2,128)(2,1)}), bf16[2,2048,1,192]{3,0,2,1:T(2,128)(2,1)S(1)}, u32[]{:S(2)}, u32[]{:S(2)}) %all-to-all-start.5) | async-done | bytes 1572896 | tf_op jit(solution)/shard_map/all_to_all | solution.py:124
  338.4 8.2 %convolution_add_fusion = f32[256,2432]{1,0:T(8,128)S(1)} fusion(bf16[2432,2432]{1,0:T(8,128)(2,1)} %param.34, bf16[304,8,2,128]{3,2,1,0:T(2,128)(2,1)S(1)} %bitcast.184, f32[2432]{0:T(1024)S(1)} %copy-done.8, pred[2432]{0:T(1024)(128)(4,1)S(1)} %copy-done.7), kind=kOutput, calls=%fused_computation.24 | convolution fusion | flops 3029532672 | bytes 15576960 | tf_op jit(solution)/shard_map/dot_general | solution.py:131
  350.0 36.1 %psum.15 = f32[2]{0:T(128)S(1)} all-reduce(f32[2]{0:T(128)S(1)} %get-tuple-element.138), channel_id=1, replica_groups=mesh['cfg'=2,'req'=4,'seq'=16] {'seq'}, use_global_device_ids=true, to_apply=%region_14.17 | all-reduce | flops 2 | bytes 16 | tf_op jit(solution)/shard_map/psum | solution.py:141
  (302 shorter events, 209.7 us)
Async XLA Ops:
  7.2 341.6 %copy-start = (bf16[2432,64]{0,1:T(8,128)(2,1)S(1)}, bf16[2432,64]{0,1:T(8,128)(2,1)}, u32[]{:S(2)}) copy-start(bf16[2432,64]{0,1:T(8,128)(2,1)} %param.38) | copy-start | bytes 933892
  8.0 7.2 %copy-start.9 = (pred[48]{0:T(512)(128)(4,1)}, pred[48]{0:T(512)(128)(4,1)S(1)}, u32[]{:S(2)}) copy-start(pred[48]{0:T(512)(128)(4,1)S(1)} %fusion.22) | copy-start | bytes 148
  10.1 14.0 %copy-start.3 = (bf16[1,2,128,2432]{3,2,1,0:T(8,128)(2,1)S(1)}, bf16[1,2,128,2432]{3,2,1,0:T(8,128)(2,1)}, u32[]{:S(2)}) copy-start(bf16[1,2,128,2432]{3,2,1,0:T(8,128)(2,1)} %param.27) | copy-start | bytes 3735556
  16.1 22.4 %all-to-all-start.2 = ((bf16[2,10,16,192]{3,0,1,2:T(2,128)(2,1)}), bf16[2,10,16,192]{3,0,1,2:T(2,128)(2,1)}, u32[]{:S(2)}, u32[]{:S(2)}) async-start(bf16[2,10,16,192]{3,0,1,2:T(2,128)(2,1)} %copy.148), calls=%async_computation.2 | async-start | bytes 327680 | tf_op jit(solution)/shard_map/all_to_all | solution.py:102
  38.5 15.4 %all-to-all-start.4 = ((bf16[2,10,16,192]{3,0,1,2:T(2,128)(2,1)}), bf16[2,10,16,192]{3,0,1,2:T(2,128)(2,1)}, u32[]{:S(2)}, u32[]{:S(2)}) async-start(bf16[2,10,16,192]{3,0,1,2:T(2,128)(2,1)} %copy.158), calls=%async_computation.4 | async-start | bytes 327680 | tf_op jit(solution)/shard_map/all_to_all | solution.py:103
  53.9 26.3 %all-to-all-start.1 = ((bf16[2,128,16,192]{1,3,0,2:T(8,128)(2,1)}), bf16[2,128,16,192]{1,3,0,2:T(8,128)(2,1)S(1)}, u32[]{:S(2)}, u32[]{:S(2)}) async-start(bf16[2,128,16,192]{1,3,0,2:T(8,128)(2,1)} %copy.144), calls=%async_computation.1 | async-start | bytes 3145728 | tf_op jit(solution)/shard_map/all_to_all | solution.py:100
  80.2 25.9 %all-to-all-start.3 = ((bf16[2,128,16,192]{1,3,0,2:T(8,128)(2,1)}), bf16[2,128,16,192]{1,3,0,2:T(8,128)(2,1)S(1)}, u32[]{:S(2)}, u32[]{:S(2)}) async-start(bf16[2,128,16,192]{1,3,0,2:T(8,128)(2,1)} %copy.154), calls=%async_computation.3 | async-start | bytes 3145728 | tf_op jit(solution)/shard_map/all_to_all | solution.py:101
  85.5 25.3 %copy-start.14 = (s32[1,2]{1,0:T(1,128)S(1)}, s32[1,2]{1,0:T(1,128)}, u32[]{:S(2)}) copy-start(s32[1,2]{1,0:T(1,128)} %param.32) | copy-start | bytes 28
  85.5 25.4 %copy-start.15 = (s32[38]{0:T(128)S(1)}, s32[38]{0:T(128)}, u32[]{:S(2)}) copy-start(s32[38]{0:T(128)} %param.33) | copy-start | bytes 460
  85.5 26.8 %copy-start.16 = (s32[2]{0:T(128)S(1)}, s32[2]{0:T(128)}, u32[]{:S(2)}) copy-start(s32[2]{0:T(128)} %param.40) | copy-start | bytes 28
  85.5 27.4 %copy-start.17 = (f32[2]{0:T(128)S(1)}, f32[2]{0:T(128)}, u32[]{:S(2)}) copy-start(f32[2]{0:T(128)} %param.41) | copy-start | bytes 28
  106.1 14.4 %copy-start.2 = (bf16[2,128,16,192]{1,3,0,2:T(8,128)(2,1)}, bf16[2,128,16,192]{1,3,0,2:T(8,128)(2,1)S(1)}, u32[]{:S(2)}) copy-start(bf16[2,128,16,192]{1,3,0,2:T(8,128)(2,1)S(1)} %all-to-all-done.3) | copy-start | bytes 4718596
  106.1 32.0 %all-to-all-start = ((bf16[2,128,16,192]{1,3,0,2:T(8,128)(2,1)}), bf16[2,128,16,192]{1,3,0,2:T(8,128)(2,1)}, u32[]{:S(2)}, u32[]{:S(2)}) async-start(bf16[2,128,16,192]{1,3,0,2:T(8,128)(2,1)} %copy.140), calls=%async_computation | async-start | bytes 3145728 | tf_op jit(solution)/shard_map/all_to_all | solution.py:99
  296.2 7.1 %copy-start.6 = (f32[1,2,2,2432]{3,2,1,0:T(2,128)S(1)}, f32[1,2,2,2432]{3,2,1,0:T(2,128)}, u32[]{:S(2)}) copy-start(f32[1,2,2,2432]{3,2,1,0:T(2,128)} %param.37) | copy-start | bytes 116740
  296.2 22.3 %copy-start.10 = (pred[48]{0:T(512)(128)(4,1)S(1)}, pred[48]{0:T(512)(128)(4,1)}, u32[]{:S(2)}) copy-start(pred[48]{0:T(512)(128)(4,1)} %copy-done.9) | copy-start | bytes 148
  296.2 34.4 %all-to-all-start.5 = ((bf16[2,2048,1,192]{3,0,2,1:T(2,128)(2,1)}), bf16[2,2048,1,192]{3,0,2,1:T(2,128)(2,1)S(1)}, u32[]{:S(2)}, u32[]{:S(2)}) async-start(bf16[2,2048,1,192]{3,0,2,1:T(2,128)(2,1)} %copy.164), calls=%async_computation.5 | async-start | bytes 4194304 | tf_op jit(solution)/shard_map/all_to_all | solution.py:124
  303.2 83.4 %all-reduce.7.cloned.1.call-start = ((), (), s32[]{:S(2)}) async-start(), calls=%async_computation.6 | async-start | bytes 131072 | tf_op jit(solution)/shard_map/psum | solution.py:161
  337.0 1.3 copy-start.7
  337.0 1.3 copy-start.8
  338.4 8.3 %copy-start.1 = (bf16[1,2,128,2432]{3,2,1,0:T(8,128)(2,1)S(1)}, bf16[1,2,128,2432]{3,2,1,0:T(8,128)(2,1)}, u32[]{:S(2)}) copy-start(bf16[1,2,128,2432]{3,2,1,0:T(8,128)(2,1)} %param.26) | copy-start | bytes 3735556
  338.4 8.3 %copy-start.4 = (f32[1,2,2432]{2,1,0:T(2,128)S(1)}, f32[1,2,2432]{2,1,0:T(2,128)}, u32[]{:S(2)}) copy-start(f32[1,2,2432]{2,1,0:T(2,128)} %param.36) | copy-start | bytes 58372
  347.9 1.4 copy-start.13
  347.9 38.7 %copy-start.5 = (f32[2,128,64]{1,2,0:T(8,128)S(1)}, f32[2,128,64]{1,2,0:T(8,128)}, u32[]{:S(2)}) copy-start(f32[2,128,64]{1,2,0:T(8,128)} %param.25) | copy-start | bytes 196612
  347.9 38.7 %copy-start.12 = (f32[2]{0:T(128)S(1)}, f32[2]{0:T(128)}, u32[]{:S(2)}) copy-start(f32[2]{0:T(128)} %divide_subtract_fusion) | copy-start | bytes 28
  (1 other events, 0.9 us)
Sparse Core Ops, SparseCore 0:
  350.2 20.4 all-reduce.6
where the time goes:
time: 399 us; the launch traced here: 396 us
  local copies, waits for them, and re-layouts  123 us (31%)
  other arithmetic  66 us (17%)
  waiting for transfers between devices  55.2 us (14%)
  blocking collectives  51.1 us (13%)
  matrix products  48.3 us (12%)
  starting transfers between devices  34.5 us (9%)
  between operations  14.5 us (4%)
  loops' own time  4.09 us (1%)
    reduce_max x24, other arithmetic, one_block(): return (result, jnp.max(row_top))  44.1 us
    psum x1, blocking collectives, local(): square_sums = lax.psum(jnp.sum(hidden * hidden, axis=(1, 2)), 'seq')  36.1 us
    all_to_all x1, waiting for transfers between devices, local(): lax.all_to_all(to_slots(streams[1]), 'seq', split_axis=2, concat_axis=1,...  21 us
    dot_general x24, matrix products, one_block(): jnp.dot(weights, all_values, preferred_element_type=jnp.float32)  20.9 us
    all_to_all x1, waiting for transfers between devices, local(): lax.all_to_all(to_slots(streams[2]), 'seq', split_axis=2, concat_axis=1,...  19.4 us
    dot_general x24, matrix products, one_block(): jnp.einsum('qd,kd->qk', query_block, all_keys, preferred_element_type=jnp...  18.7 us
    dynamic_update_slice x24, local copies, waits for them, and re-layouts, attend(): lax.map(one_block, query_rows.reshape(row_count // block_rows, block_rows...  17.5 us
    pmax x1, blocking collectives, local(): lax.pmax(jnp.max(top_scores.reshape(groups, per_shard), axis=0), ('cfg',...  15 us
  transfers between devices with their start and end apart: 7, of which 4 were waited for; matrix products, arithmetic and copies ran while one was open for 13% of the time, Pallas kernels for 0%

commit v1 on v0

v1 whole, which is shorter than its diff:
```python
import functools
import math

import jax
import jax.numpy as jnp
from jax import lax
from jax.experimental import pallas as pl
from jax.experimental.pallas import tpu as pltpu
from jax.sharding import PartitionSpec as P

STEPS = 28
LANES = 128
QT = 256
bf16 = jnp.bfloat16
f32 = jnp.float32


def sigma_of(step_idx):
    fraction = step_idx.astype(f32) / STEPS
    return 3.0 * fraction / (1.0 + 2.0 * fraction)


def pack_pairs_kernel(q_ref, k_ref, v_ref, tk_ref, tv_ref, out_ref):
    tok = q_ref.shape[2]
    txt = tk_ref.shape[2]
    for i in range(out_ref.shape[0]):
        cols = slice(i * LANES, (i + 1) * LANES)
        out_ref[i, 0:tok, :] = q_ref[0, 0, :, cols]
        out_ref[i, tok : 2 * tok, :] = k_ref[0, 0, :, cols]
        out_ref[i, 2 * tok : 3 * tok, :] = v_ref[0, 0, :, cols]
        out_ref[i, 3 * tok : 3 * tok + txt, :] = tk_ref[0, 0, :, cols]
        out_ref[i, 3 * tok + txt : 3 * tok + 2 * txt, :] = tv_ref[0, 0, :, cols]


def pack_pairs(r, q, k, v, tk, tv, shards):
    tok, txt = q.shape[2], tk.shape[2]
    rows = 3 * tok + 2 * txt
    per = 4
    img = pl.BlockSpec((1, 1, tok, per * LANES), lambda j: (0, r, 0, j))
    text = pl.BlockSpec((1, 1, txt, per * LANES), lambda j: (0, r, 0, j))
    return pl.pallas_call(
        pack_pairs_kernel,
        grid=(shards // per,),
        in_specs=[img, img, img, text, text],
        out_specs=pl.BlockSpec((per, rows, LANES), lambda j: (j, 0, 0)),
        out_shape=jax.ShapeDtypeStruct((shards, rows, LANES), bf16),
        cost_estimate=pl.CostEstimate(flops=0, bytes_accessed=4 * shards * rows * LANES, transcendentals=0),
        name="pack_pairs",
    )(q, k, v, tk, tv)


def pack_single_kernel(n_pairs, q_ref, k_ref, v_ref, tk_ref, tv_ref, out_ref):
    j = pl.program_id(0)
    tok = q_ref.shape[2]
    txt = tk_ref.shape[2]
    half = tok // 2
    hd = LANES // 2

    @pl.when(j < n_pairs)
    def _():
        for r in range(2):
            for h in range(2):
                d = 2 * r + h
                for n, ref in enumerate((q_ref, k_ref, v_ref)):
                    x = ref[0, r]
                    top, low = x[:half], x[half:]
                    if h == 0:
                        folded = jnp.concatenate([top[:, :hd], low[:, :hd]], axis=1)
                    else:
                        folded = jnp.concatenate([top[:, hd:], low[:, hd:]], axis=1)
                    out_ref[d, n * half : (n + 1) * half, :] = folded
                for n, ref in enumerate((tk_ref, tv_ref)):
                    x = ref[0, r][:, h * hd : (h + 1) * hd]
                    base = 3 * half + n * txt
                    out_ref[d, base : base + txt, :] = jnp.concatenate([x, x], axis=1)

    @pl.when(j >= n_pairs)
    def _():
        out_ref[...] = jnp.zeros_like(out_ref)


def pack_single(q, k, v, tk, tv, shards):
    tok, txt = q.shape[2], tk.shape[2]
    n_pairs = q.shape[3] // LANES - shards
    rows = 3 * (tok // 2) + 2 * txt
    last = n_pairs - 1
    img = pl.BlockSpec((1, 2, tok, LANES), lambda j: (0, 0, 0, shards + jnp.minimum(j, last)))
    text = pl.BlockSpec((1, 2, txt, LANES), lambda j: (0, 0, 0, shards + jnp.minimum(j, last)))
    return pl.pallas_call(
        functools.partial(pack_single_kernel, n_pairs),
        grid=(shards // 4,),
        in_specs=[img, img, img, text, text],
        out_specs=pl.BlockSpec((4, rows, LANES), lambda j: (j, 0, 0)),
        out_shape=jax.ShapeDtypeStruct((shards, rows, LANES), bf16),
        cost_estimate=pl.CostEstimate(flops=0, bytes_accessed=4 * shards * rows * LANES, transcendentals=0),
        name="pack_single",
    )(q, k, v, tk, tv)


def attend_kernel(folded, tok, txt, len_ref, r_ref, o_ref, top_ref, k2, vt, top):
    shards = r_ref.shape[0]
    hd = LANES // 2
    rows = tok // 2 if folded else tok
    n_img = shards * tok
    slot = 16
    n_txt = shards * slot
    t = pl.program_id(0)
    length = len_ref[0]

    @pl.when(t == 0)
    def _prep():
        for s in range(shards):
            kb = r_ref[s, rows : 2 * rows, :]
            at = slice(s * rows, (s + 1) * rows)
            k2[at, 0:LANES] = kb
            k2[at, LANES:] = kb
            if folded:
                other = jnp.concatenate([kb[:, hd:], kb[:, :hd]], axis=1)
                at2 = slice(n_img // 2 + s * rows, n_img // 2 + (s + 1) * rows)
                k2[at2, 0:LANES] = other
                k2[at2, LANES:] = other
        step = LANES // rows
        for u in range(shards // step):
            vb = r_ref[u * step : (u + 1) * step, 2 * rows : 3 * rows, :].reshape(LANES, LANES)
            vb = vb.astype(f32).T.astype(bf16)
            at = slice(u * LANES, (u + 1) * LANES)
            vt[0, 0:hd, at] = vb[:hd]
            vt[1, 0:hd, at] = vb[hd:]
            if folded:
                at2 = slice(n_img // 2 + u * LANES, n_img // 2 + (u + 1) * LANES)
                vt[0, 0:hd, at2] = vb[hd:]
                vt[1, 0:hd, at2] = vb[:hd]
        tks, tvs = [], []
        pad = jnp.zeros((slot - txt, LANES), f32)
        for s in range(shards):
            tks += [r_ref[s, 3 * rows : 3 * rows + txt, :].astype(f32), pad]
            tvs += [r_ref[s, 3 * rows + txt : 3 * rows + 2 * txt, :].astype(f32), pad]
        tkx = jnp.concatenate(tks, axis=0)
        tvx = jnp.concatenate(tvs, axis=0)
        i = lax.broadcasted_iota(jnp.int32, (n_txt, LANES), 0)
        live = ((i % slot) < txt) & ((i // slot) * txt + (i % slot) < length)
        key0 = k2[0:16, 0:LANES].astype(f32)[0:1]
        tkx = jnp.where(live, tkx, jnp.broadcast_to(key0, (n_txt, LANES))).astype(bf16)
        k2[n_img:, 0:LANES] = tkx
        k2[n_img:, LANES:] = tkx
        tvx = jnp.where(live, tvx, 0.0)
        for u in range(n_txt // LANES):
            vb = tvx[u * LANES : (u + 1) * LANES].T.astype(bf16)
            at = slice(n_img + u * LANES, n_img + (u + 1) * LANES)
            vt[0, 0:hd, at] = vb[:hd]
            vt[1, 0:hd, at] = vb[hd:]
        c = lax.broadcasted_iota(jnp.int32, (slot, n_txt), 1)
        live_t = ((c % slot) < txt) & ((c // slot) * txt + (c % slot) < length)
        ones_t = jnp.where(live_t, 1.0, 0.0).astype(bf16)
        for h in range(2):
            vt[h, hd:, 0:n_img] = jnp.ones((slot, n_img), bf16)
            vt[h, hd:, n_img:] = ones_t
        top[...] = jnp.full(top.shape, -jnp.inf, f32)

    per = QT // rows
    q = r_ref[pl.ds(t * per, per), 0:rows, :].reshape(QT, LANES).astype(f32)
    q = q * (math.log2(math.e) / math.sqrt(hd))
    lane = lax.broadcasted_iota(jnp.int32, (QT, LANES), 1)
    outs = []
    for h in range(2):
        qh = jnp.where((lane >= hd) == (h == 1), q, 0.0)
        hi = qh.astype(bf16)
        lo = (qh - hi.astype(f32)).astype(bf16)
        q2 = jnp.concatenate([hi, lo], axis=1)
        s = lax.dot_general(k2[...], q2, (((1,), (1,)), ((), ())), preferred_element_type=f32)
        m = jnp.max(s, axis=0, keepdims=True)
        p = jnp.exp2(s - m).astype(bf16)
        o = jnp.dot(vt[h], p, preferred_element_type=f32)
        outs.append(o[:hd] / o[hd : hd + 1])
        top[h : h + 1, :] = jnp.maximum(top[h : h + 1, :], m)
    out = jnp.concatenate(outs, axis=0).T.astype(bf16)
    o_ref[...] = out.reshape(per, rows, LANES)

    @pl.when(t == pl.num_programs(0) - 1)
    def _fin():
        best = jnp.max(top[...], axis=1, keepdims=True) * math.log(2.0)
        top_ref[...] = jnp.broadcast_to(best, top_ref.shape)


def attend(received, length, tok, txt, folded):
    shards, total, _ = received.shape
    rows = tok // 2 if folded else tok
    n_keys = shards * (tok + 16)
    per = QT // rows
    heads = 1 if folded else 2
    return pl.pallas_call(
        functools.partial(attend_kernel, folded, tok, txt),
        grid=(shards // per,),
        in_specs=[
            pl.BlockSpec(memory_space=pltpu.SMEM),
            pl.BlockSpec((shards, total, LANES), lambda t: (0, 0, 0)),
        ],
        out_specs=[
            pl.BlockSpec((per, rows, LANES), lambda t: (t, 0, 0)),
            pl.BlockSpec((8, LANES), lambda t: (0, 0)),
        ],
        out_shape=[
            jax.ShapeDtypeStruct((shards, rows, LANES), bf16),
            jax.ShapeDtypeStruct((8, LANES), f32),
        ],
        scratch_shapes=[
            pltpu.VMEM((n_keys, 2 * LANES), bf16),
            pltpu.VMEM((2, LANES // 2 + 16, n_keys), bf16),
            pltpu.VMEM((8, QT), f32),
        ],
        compiler_params=pltpu.CompilerParams(vmem_limit_bytes=40 * 1024 * 1024),
        cost_estimate=pl.CostEstimate(
            flops=heads * 4 * shards * tok * n_keys * LANES,
            bytes_accessed=4 * shards * total * LANES,
            transcendentals=heads * shards * tok * n_keys,
        ),
        name="attend_single" if folded else "attend_pair",
    )(length, received)


def finish_kernel(
    n_pairs, half_ref, a_ref, b_ref, c_ref, hid_ref, gate_ref, mod_ref, ob_ref, fw_ref, fb_ref, w_hbm,
    pred_ref, sq_ref, att, w, acc, sem,
):
    shards, tok, _ = a_ref.shape
    width = w.shape[0]
    hd = LANES // 2
    half = tok // 2
    edges = list(range(0, width, 4 * LANES)) + [width]
    copies = [
        pltpu.make_async_copy(w_hbm.at[lo:up, :], w.at[lo:up, :], sem.at[n])
        for n, (lo, up) in enumerate(zip(edges[:-1], edges[1:]))
    ]
    for copy in copies:
        copy.start()
    for d in range(shards):
        att[0:tok, d * LANES : (d + 1) * LANES] = a_ref[d]
        att[tok:, d * LANES : (d + 1) * LANES] = b_ref[d]
    for j in range(n_pairs):
        for r in range(2):
            x0 = c_ref[4 * j + 2 * r]
            x1 = c_ref[4 * j + 2 * r + 1]
            cols = slice((shards + j) * LANES, (shards + j + 1) * LANES)
            att[r * tok : r * tok + half, cols] = jnp.concatenate([x0[:, :hd], x1[:, :hd]], axis=1)
            att[r * tok + half : (r + 1) * tok, cols] = jnp.concatenate([x0[:, hd:], x1[:, hd:]], axis=1)
    for n, (lo, up) in enumerate(zip(edges[:-1], edges[1:])):
        copies[n].wait()
        part = jnp.dot(att[:, lo:up], w[lo:up, :], preferred_element_type=f32)
        if n == 0:
            acc[...] = part
        else:
            acc[...] += part

    step = 16
    for r in range(2):
        gate = gate_ref[0, r : r + 1, :]
        shift = mod_ref[0, r, 0:1, :]
        scale = 1.0 + mod_ref[0, r, 1:2, :]
        bias = ob_ref[...]

        def body(i, total):
            at = pl.ds(r * tok + i * step, step)
            hid = hid_ref[0, r, pl.ds(i * step, step), :].astype(f32) + gate * (acc[at, :] + bias)
            total = total + jnp.sum(hid * hid, axis=1, keepdims=True)
            mean = jnp.mean(hid, axis=1, keepdims=True)
            cen = hid - mean
            var = jnp.mean(cen * cen, axis=1, keepdims=True)
            att[at, :] = (cen / jnp.sqrt(var + 1e-6) * scale + shift).astype(bf16)
            return total

        total = lax.fori_loop(0, tok // step, body, jnp.zeros((step, 1), f32))
        sq_ref[r : r + 1, :] = jnp.broadcast_to(jnp.sum(total, axis=0, keepdims=True), (1, LANES))
        pred = jnp.dot(att[r * tok : (r + 1) * tok, :], fw_ref[...], preferred_element_type=f32)
        pred_ref[r] = half_ref[r] * (pred + fb_ref[...])


def finish(half_weight, ra, rb, rc, hidden_in, gate, mod, out_bias, final_weight, final_bias, out_weight):
    shards, tok, _ = ra.shape
    width = out_weight.shape[0]
    c_out = final_weight.shape[1]
    n_pairs = width // LANES - shards
    vmem = pl.BlockSpec(memory_space=pltpu.VMEM)
    return pl.pallas_call(
        functools.partial(finish_kernel, n_pairs),
        in_specs=[pl.BlockSpec(memory_space=pltpu.SMEM)] + [vmem] * 9 + [pl.BlockSpec(memory_space=pl.ANY)],
        out_specs=[vmem, vmem],
        out_shape=[
            jax.ShapeDtypeStruct((2, tok, c_out), f32),
            jax.ShapeDtypeStruct((8, LANES), f32),
        ],
        scratch_shapes=[
            pltpu.VMEM((2 * tok, width), bf16),
            pltpu.VMEM((width, width), bf16),
            pltpu.VMEM((2 * tok, width), f32),
            pltpu.SemaphoreType.DMA((5,)),
        ],
        compiler_params=pltpu.CompilerParams(vmem_limit_bytes=40 * 1024 * 1024),
        cost_estimate=pl.CostEstimate(
            flops=4 * tok * width * (width + c_out), bytes_accessed=2 * width * width, transcendentals=0
        ),
        name="finish",
    )(half_weight, ra, rb, rc, hidden_in, gate, mod, out_bias, final_weight, final_bias, out_weight)


def ring_stage(x, axis, size, move, combine):
    pairs = [[(i, move(i, k)) for i in range(size)] for k in (1, 2, 3)]
    others = [lax.ppermute(x, axis, p) for p in pairs]
    return combine(combine(x, others[0]), combine(others[1], others[2]))


def local(
    latent, hidden_in, img_query, img_key, img_value, txt_key, txt_value, text_len, head_slot,
    out_weight, out_bias, attn_gate, final_mod, final_weight, final_bias, timesteps, guidance,
):
    shards = lax.axis_size("seq")
    position = lax.axis_index("seq")
    head_count = head_slot.shape[0]
    model_width = out_weight.shape[0]
    tok, txt = img_query.shape[2], txt_key.shape[2]
    image_rows = tok * shards
    per_shard = (head_count + shards - 1) // shards

    streams = (img_query, img_key, img_value, txt_key, txt_value)

    def swap(x):
        return lax.all_to_all(x, "seq", split_axis=0, concat_axis=0, tiled=True)

    lengths = text_len[0]
    length_c = jnp.where((position % 4) // 2 == 0, lengths[0], lengths[1])

    in_a = swap(pack_pairs(0, *streams, shards))
    in_b = swap(pack_pairs(1, *streams, shards))
    in_c = swap(pack_single(*streams, shards))
    out_a, top_a = attend(in_a, lengths[0:1], tok, txt, False)
    back_a = swap(out_a)
    out_b, top_b = attend(in_b, lengths[1:2], tok, txt, False)
    back_b = swap(out_b)
    out_c, top_c = attend(in_c, length_c[None], tok, txt, True)
    back_c = swap(out_c)

    half_weight = jnp.where(lax.axis_index("cfg") == 0, guidance, 1.0 - guidance)
    pred, squares = finish(
        half_weight, back_a, back_b, back_c, hidden_in, attn_gate, final_mod,
        out_bias[None], final_weight, final_bias[None], out_weight,
    )
    velocity = pred + lax.ppermute(pred, "cfg", [(0, 1), (1, 0)])
    step_size = (sigma_of(timesteps - 1) - sigma_of(timesteps))[:, None, None]
    latent_next = latent + step_size * velocity

    lane = jnp.arange(LANES, dtype=jnp.int32)
    pair_top = jnp.maximum(top_a[0:2, 0], top_b[0:2, 0])
    single_top = jnp.maximum(top_c[0, 0], top_c[1, 0])
    single_head = 2 * shards + 2 * (position // 4) + position % 2
    table = jnp.full((LANES,), -jnp.inf, f32)
    table = jnp.where(lane == 2 * position, pair_top[0], table)
    table = jnp.where(lane == 2 * position + 1, pair_top[1], table)
    table = jnp.where((lane == single_head) & (single_head < head_count), single_top, table)
    table = jnp.maximum(table, lax.ppermute(table, "cfg", [(0, 1), (1, 0)]))
    table = ring_stage(table, "req", 4, lambda i, k: (i + k) % 4, jnp.maximum)

    small = jnp.concatenate([table[: LANES - 2], squares[0:2, 0]])

    def combine(a, b):
        return jnp.where(lane < LANES - 2, jnp.maximum(a, b), a + b)

    small = ring_stage(small, "seq", shards, lambda i, k: i // 4 * 4 + (i + k) % 4, combine)
    small = ring_stage(small, "seq", shards, lambda i, k: (i + 4 * k) % shards, combine)
    hidden_norms = jnp.sqrt(small[LANES - 2 :] / (image_rows * model_width))[None, :]

    own_slots = position * per_shard + jnp.arange(per_shard, dtype=jnp.int32)
    match = head_slot[None, :] == own_slots[:, None]
    best = jnp.max(jnp.where(match, small[None, :head_count], -jnp.inf), axis=1)
    max_logits = jnp.where(jnp.any(match, axis=1), best, 0.0)
    return (velocity, latent_next, hidden_norms, max_logits)


def solution(mesh):
    in_specs = (
        P("req", "seq", None),
        P("cfg", "req", "seq", None),
        P("cfg", "req", "seq", None),
        P("cfg", "req", "seq", None),
        P("cfg", "req", "seq", None),
        P("cfg", "req", "seq", None),
        P("cfg", "req", "seq", None),
        P("cfg", "req"),
        P(),
        P(),
        P(),
        P("cfg", "req", None),
        P("cfg", "req", None, None),
        P(),
        P(),
        P("req"),
        P("req"),
    )
    out_specs = (P("req", "seq", None), P("req", "seq", None), P("cfg", "req"), P("seq"))
    return jax.shard_map(local, mesh=mesh, in_specs=in_specs, out_specs=out_specs, check_vma=False)
```

time: 399 us -> 199 us (0.50)
  local copies, waits for them, and re-layouts: 123 us -> 11.5 us
  Pallas kernels: 0 us -> 83.4 us
  other arithmetic: 66 us -> 4.27 us
  blocking collectives: 51.1 us -> 0 us
  matrix products: 48.3 us -> 0 us
  starting transfers between devices: 34.5 us -> 49.8 us
  between operations: 14.5 us -> 3.58 us
  waiting for transfers between devices: 55.2 us -> 45.7 us
  loops' own time: 4.09 us -> 0 us
    pallas_call x0 -> x7, Pallas kernels: none -> 83.4 us  [the longest x3 61.6 us: attend(): pl.pallas_call(functools.partial(attend_kernel, folded, tok, txt), grid=(...]
    dot_general x50 -> x0, matrix products: 48.3 us -> none  [the longest x24 20.9 us: one_block(): jnp.dot(weights, all_values, preferred_element_type=jnp.float32)]
    reduce_max x31 -> x1, other arithmetic: 48.1 us -> 0.18 us  [local(): best = jnp.max(jnp.where(match, small[None, :head_count], -jnp.inf), axis=1)]
    psum x1 -> x0, blocking collectives: 36.1 us -> none  [local(): square_sums = lax.psum(jnp.sum(hidden * hidden, axis=(1, 2)), 'seq')]
    reshape x19 -> x0, local copies, waits for them, and re-layouts: 36 us -> none  [the longest x5 13.2 us: by_slot(): tensor.reshape(groups, row_count, per_shard, head_dim).transpose(0, 2, 1, 3)]
    dynamic_update_slice x42 -> x0, local copies, waits for them, and re-layouts: 27.5 us -> none  [the longest x24 17.5 us: attend(): lax.map(one_block, query_rows.reshape(row_count // block_rows, block_rows...]
    ppermute x0 -> x11, starting transfers between devices: none -> 16.4 us  [the longest x9 16.2 us: ring_stage(): others = [lax.ppermute(x, axis, p) for p in pairs]]
    pmax x1 -> x0, blocking collectives: 15 us -> none  [local(): lax.pmax(jnp.max(top_scores.reshape(groups, per_shard), axis=0), ('cfg',...]
  transfers between devices with their start and end apart: 7 -> 17, of which waited for: 4 -> 9; matrix products, arithmetic and copies ran while one was open for 13% -> 4% of each run, Pallas kernels for 0% -> 35%
where the time goes in v1:
time: 199 us; the launch traced here: 198 us
  Pallas kernels  83.4 us (42%)
  starting transfers between devices  49.8 us (25%)
  waiting for transfers between devices  45.7 us (23%)
  local copies, waits for them, and re-layouts  11.5 us (6%)
  other arithmetic  4.27 us (2%)
  between operations  3.58 us (2%)
    pallas_call x3, Pallas kernels, attend(): pl.pallas_call(functools.partial(attend_kernel, folded, tok, txt), grid=(...  61.6 us
    all_to_all x6, waiting for transfers between devices, swap(): return lax.all_to_all(x, 'seq', split_axis=0, concat_axis=0, tiled=True)  40.4 us
    all_to_all x6, starting transfers between devices, swap(): return lax.all_to_all(x, 'seq', split_axis=0, concat_axis=0, tiled=True)  33.4 us
    ppermute x9, starting transfers between devices, ring_stage(): others = [lax.ppermute(x, axis, p) for p in pairs]  16.2 us
    pallas_call x1, Pallas kernels, finish(): pl.pallas_call(functools.partial(finish_kernel, n_pairs), in_specs=[pl.Bl...  11.2 us
    unnamed x36, local copies, waits for them, and re-layouts  9.71 us
    pallas_call x2, Pallas kernels, pack_pairs(): pl.pallas_call(pack_pairs_kernel, grid=(shards // per,), in_specs=[img, i...  7.55 us
    ppermute x9, waiting for transfers between devices, ring_stage(): others = [lax.ppermute(x, axis, p) for p in pairs]  5.29 us
  transfers between devices with their start and end apart: 17, of which 9 were waited for; matrix products, arithmetic and copies ran while one was open for 4% of the time, Pallas kernels for 35%

profile of v1, /device:TPU:0, one launch (start us, length us, event | category | flops | bytes accessed | tf_op | source)
XLA Modules:
  0.0 198.3 jit_solution(12595433892038627396)
XLA Ops:
  0.6 1.6 copy.41.tk_ref
  2.2 1.6 copy.42.tv_ref
  3.8 3.1 %pack_single.1 = bf16[16,212,128]{2,1,0:T(8,128)(2,1)} custom-call(bf16[1,2,128,2432]{3,2,1,0:T(8,128)(2,1)} %q_ref.5, bf16[1,2,128,2432]{3,2,1,0:T(8,128)(2,1)} %k_ref.5, bf16[1,2,128,2432]{3,2,1,0:T(8,128)(2,1)} %v_ref.5, bf16[1,2,10,2432]{3,2,1,0:T(8,128)(2,1)} %copy.41.tk_ref, bf16[1,2,10,2432]{3,2,1,0:T(8,128)(2,1)} %copy.42.tv_ref), custom_call_target="tpu_custom_call" | custom-call | bytes 1736704 | tf_op jit(solution)/shard_map/pack_single/pallas_call | solution.py:89
  6.8 8.0 %all-to-all-start.4 = ((bf16[16,212,128]{2,1,0:T(8,128)(2,1)}), bf16[16,212,128]{2,1,0:T(8,128)(2,1)S(1)}, u32[]{:S(2)}, u32[]{:S(2)}) async-start(bf16[16,212,128]{2,1,0:T(8,128)(2,1)} %pack_single.1), calls=%async_computation.4 | async-start | bytes 1769472 | tf_op jit(solution)/shard_map/all_to_all | solution.py:326
  14.8 3.8 %pack_pairs.2 = bf16[16,404,128]{2,1,0:T(8,128)(2,1)} custom-call(bf16[1,2,128,2432]{3,2,1,0:T(8,128)(2,1)} %q_ref.5, bf16[1,2,128,2432]{3,2,1,0:T(8,128)(2,1)} %k_ref.5, bf16[1,2,128,2432]{3,2,1,0:T(8,128)(2,1)} %v_ref.5, bf16[1,2,10,2432]{3,2,1,0:T(8,128)(2,1)} %copy.41.tk_ref, bf16[1,2,10,2432]{3,2,1,0:T(8,128)(2,1)} %copy.42.tv_ref), custom_call_target="tpu_custom_call" | custom-call | bytes 3309568 | tf_op jit(solution)/shard_map/pack_pairs/pallas_call | solution.py:41
  18.6 11.9 %all-to-all-done.4.r_ref = bf16[16,212,128]{2,1,0:T(8,128)(2,1)S(1)} async-done(((bf16[16,212,128]{2,1,0:T(8,128)(2,1)}), bf16[16,212,128]{2,1,0:T(8,128)(2,1)S(1)}, u32[]{:S(2)}, u32[]{:S(2)}) %all-to-all-start.4) | async-done | bytes 868384 | tf_op jit(solution)/shard_map/all_to_all | solution.py:326
  31.4 3.7 %all-to-all-start = ((bf16[16,404,128]{2,1,0:T(8,128)(2,1)}), bf16[16,404,128]{2,1,0:T(8,128)(2,1)S(1)}, u32[]{:S(2)}, u32[]{:S(2)}) async-start(bf16[16,404,128]{2,1,0:T(8,128)(2,1)} %pack_pairs.2), calls=%async_computation | async-start | bytes 3342336 | tf_op jit(solution)/shard_map/all_to_all | solution.py:326
  35.1 3.8 %pack_pairs.3 = bf16[16,404,128]{2,1,0:T(8,128)(2,1)} custom-call(bf16[1,2,128,2432]{3,2,1,0:T(8,128)(2,1)} %q_ref.5, bf16[1,2,128,2432]{3,2,1,0:T(8,128)(2,1)} %k_ref.5, bf16[1,2,128,2432]{3,2,1,0:T(8,128)(2,1)} %v_ref.5, bf16[1,2,10,2432]{3,2,1,0:T(8,128)(2,1)} %copy.41.tk_ref, bf16[1,2,10,2432]{3,2,1,0:T(8,128)(2,1)} %copy.42.tv_ref), custom_call_target="tpu_custom_call" | custom-call | bytes 3309568 | tf_op jit(solution)/shard_map/pack_pairs/pallas_call | solution.py:41
  38.9 19.7 %all-to-all-done.r_ref = bf16[16,404,128]{2,1,0:T(8,128)(2,1)S(1)} async-done(((bf16[16,404,128]{2,1,0:T(8,128)(2,1)}), bf16[16,404,128]{2,1,0:T(8,128)(2,1)S(1)}, u32[]{:S(2)}, u32[]{:S(2)}) %all-to-all-start) | async-done | bytes 1654816 | tf_op jit(solution)/shard_map/all_to_all | solution.py:326
  58.6 3.7 %all-to-all-start.2 = ((bf16[16,404,128]{2,1,0:T(8,128)(2,1)}), bf16[16,404,128]{2,1,0:T(8,128)(2,1)S(1)}, u32[]{:S(2)}, u32[]{:S(2)}) async-start(bf16[16,404,128]{2,1,0:T(8,128)(2,1)} %pack_pairs.3), calls=%async_computation.2 | async-start | bytes 3342336 | tf_op jit(solution)/shard_map/all_to_all | solution.py:326
  65.4 12.2 %attend_single.1 = (bf16[16,64,128]{2,1,0:T(8,128)(2,1)S(1)}, f32[8,128]{1,0:T(8,128)S(1)}) custom-call(s32[1]{0:T(128)} %bitcast.4.len_ref, bf16[16,212,128]{2,1,0:T(8,128)(2,1)S(1)} %copy-done.2), custom_call_target="tpu_custom_call" | custom-call | flops 2415919104 | bytes 1736704 | tf_op jit(solution)/shard_map/attend_single/pallas_call | solution.py:191
  79.5 24.7 %attend_pair.2 = (bf16[16,128,128]{2,1,0:T(8,128)(2,1)S(1)}, f32[8,128]{1,0:T(8,128)S(1)}) custom-call(s32[1]{0:T(128)} %bitcast.len_ref, bf16[16,404,128]{2,1,0:T(8,128)(2,1)S(1)} %all-to-all-done.r_ref), custom_call_target="tpu_custom_call" | custom-call | flops 4831838208 | bytes 3309568 | tf_op jit(solution)/shard_map/attend_pair/pallas_call | solution.py:191
  105.0 7.1 %all-to-all-start.5 = ((bf16[16,64,128]{2,1,0:T(8,128)(2,1)}), bf16[16,64,128]{2,1,0:T(8,128)(2,1)S(1)}, u32[]{:S(2)}, u32[]{:S(2)}) async-start(bf16[16,64,128]{2,1,0:T(8,128)(2,1)} %copy-done.5), calls=%async_computation.5 | async-start | bytes 524288 | tf_op jit(solution)/shard_map/all_to_all | solution.py:326
  112.1 24.7 %attend_pair.3 = (bf16[16,128,128]{2,1,0:T(8,128)(2,1)S(1)}, f32[8,128]{1,0:T(8,128)S(1)}) custom-call(s32[1]{0:T(128)} %bitcast.1.len_ref, bf16[16,404,128]{2,1,0:T(8,128)(2,1)S(1)} %all-to-all-done.2.r_ref), custom_call_target="tpu_custom_call" | custom-call | flops 4831838208 | bytes 3309568 | tf_op jit(solution)/shard_map/attend_pair/pallas_call | solution.py:191
  137.7 7.4 %all-to-all-start.1 = ((bf16[16,128,128]{2,1,0:T(8,128)(2,1)}), bf16[16,128,128]{2,1,0:T(8,128)(2,1)S(1)}, u32[]{:S(2)}, u32[]{:S(2)}) async-start(bf16[16,128,128]{2,1,0:T(8,128)(2,1)} %copy-done.4), calls=%async_computation.1 | async-start | bytes 1048576 | tf_op jit(solution)/shard_map/all_to_all | solution.py:326
  147.0 8.2 %all-to-all-done.1.a_ref = bf16[16,128,128]{2,1,0:T(8,128)(2,1)S(1)} async-done(((bf16[16,128,128]{2,1,0:T(8,128)(2,1)}), bf16[16,128,128]{2,1,0:T(8,128)(2,1)S(1)}, u32[]{:S(2)}, u32[]{:S(2)}) %all-to-all-start.1) | async-done | bytes 524320 | tf_op jit(solution)/shard_map/all_to_all | solution.py:326
  155.2 3.6 %all-to-all-start.3 = ((bf16[16,128,128]{2,1,0:T(8,128)(2,1)}), bf16[16,128,128]{2,1,0:T(8,128)(2,1)S(1)}, u32[]{:S(2)}, u32[]{:S(2)}) async-start(bf16[16,128,128]{2,1,0:T(8,128)(2,1)} %copy-done.3), calls=%async_computation.3 | async-start | bytes 1048576 | tf_op jit(solution)/shard_map/all_to_all | solution.py:326
  160.1 1.6 collective-permute-start.2
  161.7 2.9 %collective-permute-start.3 = (f32[128]{0:T(128)S(1)}, f32[128]{0:T(128)S(1)}, u32[]{:S(2)}, u32[]{:S(2)}) collective-permute-start(f32[128]{0:T(128)S(1)} %fusion.4), channel_id=1, source_target_pairs={{0,32},{16,48},{32,0},{48,16},{1,33},{17,49},{33,1},{49,17},{2,34}... | collective-permute-start | bytes 1544 | tf_op jit(solution)/shard_map/ppermute | solution.py:307
  168.9 11.2 %finish.1 = (f32[2,128,64]{2,1,0:T(8,128)S(1)}, f32[8,128]{1,0:T(8,128)S(1)}) custom-call(f32[2]{0:T(128)S(1)} %broadcast_select_fusion.half_ref, bf16[16,128,128]{2,1,0:T(8,128)(2,1)S(1)} %all-to-all-done.1.a_ref, bf16[16,128,128]{2,1,0:T(8,128)(2,1)S(1)} %all-to-all-done.3.b_ref, bf16[16,64,128]{2,1,0:T(8,128)(2,1)S(1)} %all-to-all-done.5.c_ref, ...), custom_call_target="tpu_custom_call" | custom-call | flops 3107979264 | bytes 11829248 | tf_op jit(solution)/shard_map/finish/pallas_call | solution.py:283
  181.5 2.7 %collective-permute-start.6 = (f32[128]{0:T(128)S(1)}, f32[128]{0:T(128)S(1)}, u32[]{:S(2)}, u32[]{:S(2)}) collective-permute-start(f32[128]{0:T(128)S(1)} %pad_maximum_fusion), channel_id=1, source_target_pairs={{0,2},{1,3},{2,0},{3,1},{4,6},{5,7},{6,4},{7,5},{8,10},{9,11},{10,... | collective-permute-start | bytes 1544 | tf_op jit(solution)/shard_map/ppermute | solution.py:307
  187.7 2.8 %collective-permute-start.10 = (f32[128]{0:T(128)S(1)}, f32[128]{0:T(128)S(1)}, u32[]{:S(2)}, u32[]{:S(2)}) collective-permute-start(f32[128]{0:T(128)S(1)} %add_select_fusion.1), channel_id=1, source_target_pairs={{0,12},{1,13},{2,14},{3,15},{4,0},{5,1},{6,2},{7,3},{8,4},{9,5},{1... | collective-permute-start | bytes 1544 | tf_op jit(solution)/shard_map/ppermute | solution.py:307
  190.5 2.3 %collective-permute-start.9 = (f32[128]{0:T(128)S(1)}, f32[128]{0:T(128)S(1)}, u32[]{:S(2)}, u32[]{:S(2)}) collective-permute-start(f32[128]{0:T(128)S(1)} %add_select_fusion.1), channel_id=1, source_target_pairs={{0,8},{1,9},{2,10},{3,11},{4,12},{5,13},{6,14},{7,15},{8,0},{9,1},... | collective-permute-start | bytes 1544 | tf_op jit(solution)/shard_map/ppermute | solution.py:307
  193.2 2.1 %collective-permute-done.8 = f32[128]{0:T(128)S(1)} collective-permute-done((f32[128]{0:T(128)S(1)}, f32[128]{0:T(128)S(1)}, u32[]{:S(2)}, u32[]{:S(2)}) %collective-permute-start.8) | collective-permute-done | bytes 544 | tf_op jit(solution)/shard_map/ppermute | solution.py:307
  (73 shorter events, 20.7 us)
Async XLA Ops:
  6.8 23.6 %all-to-all-start.4 = ((bf16[16,212,128]{2,1,0:T(8,128)(2,1)}), bf16[16,212,128]{2,1,0:T(8,128)(2,1)S(1)}, u32[]{:S(2)}, u32[]{:S(2)}) async-start(bf16[16,212,128]{2,1,0:T(8,128)(2,1)} %pack_single.1), calls=%async_computation.4 | async-start | bytes 1769472 | tf_op jit(solution)/shard_map/all_to_all | solution.py:326
  31.4 27.2 %all-to-all-start = ((bf16[16,404,128]{2,1,0:T(8,128)(2,1)}), bf16[16,404,128]{2,1,0:T(8,128)(2,1)S(1)}, u32[]{:S(2)}, u32[]{:S(2)}) async-start(bf16[16,404,128]{2,1,0:T(8,128)(2,1)} %pack_pairs.2), calls=%async_computation | async-start | bytes 3342336 | tf_op jit(solution)/shard_map/all_to_all | solution.py:326
  58.6 46.4 %all-to-all-start.2 = ((bf16[16,404,128]{2,1,0:T(8,128)(2,1)}), bf16[16,404,128]{2,1,0:T(8,128)(2,1)S(1)}, u32[]{:S(2)}, u32[]{:S(2)}) async-start(bf16[16,404,128]{2,1,0:T(8,128)(2,1)} %pack_pairs.3), calls=%async_computation.2 | async-start | bytes 3342336 | tf_op jit(solution)/shard_map/all_to_all | solution.py:326
  105.0 32.7 %all-to-all-start.5 = ((bf16[16,64,128]{2,1,0:T(8,128)(2,1)}), bf16[16,64,128]{2,1,0:T(8,128)(2,1)S(1)}, u32[]{:S(2)}, u32[]{:S(2)}) async-start(bf16[16,64,128]{2,1,0:T(8,128)(2,1)} %copy-done.5), calls=%async_computation.5 | async-start | bytes 524288 | tf_op jit(solution)/shard_map/all_to_all | solution.py:326
  112.1 34.9 %copy-start.13 = (s32[2]{0:T(128)S(1)}, s32[2]{0:T(128)}, u32[]{:S(2)}) copy-start(s32[2]{0:T(128)} %param.32) | copy-start | bytes 28
  137.6 28.4 %copy-start.14 = (f32[2]{0:T(128)S(1)}, f32[2]{0:T(128)}, u32[]{:S(2)}) copy-start(f32[2]{0:T(128)} %param.33) | copy-start | bytes 28
  137.6 29.6 %copy-start.10 = (f32[2432]{0:T(1024)S(1)}, f32[2432]{0:T(1024)}, u32[]{:S(2)}) copy-start(f32[2432]{0:T(1024)} %param.27) | copy-start | bytes 29188
  137.6 31.2 %copy-start = (bf16[1,2,128,2432]{3,2,1,0:T(8,128)(2,1)S(1)}, bf16[1,2,128,2432]{3,2,1,0:T(8,128)(2,1)}, u32[]{:S(2)}) copy-start(bf16[1,2,128,2432]{3,2,1,0:T(8,128)(2,1)} %hid_ref.1) | copy-start | bytes 3735556
  137.6 31.2 %copy-start.6 = (f32[1,2,2,2432]{3,2,1,0:T(2,128)S(1)}, f32[1,2,2,2432]{3,2,1,0:T(2,128)}, u32[]{:S(2)}) copy-start(f32[1,2,2,2432]{3,2,1,0:T(2,128)} %mod_ref.1) | copy-start | bytes 116740
  137.7 31.2 %copy-start.7 = (f32[1,2,2432]{2,1,0:T(2,128)S(1)}, f32[1,2,2432]{2,1,0:T(2,128)}, u32[]{:S(2)}) copy-start(f32[1,2,2432]{2,1,0:T(2,128)} %gate_ref.1) | copy-start | bytes 58372
  137.7 31.2 %copy-start.8 = (f32[64]{0:T(128)S(1)}, f32[64]{0:T(128)}, u32[]{:S(2)}) copy-start(f32[64]{0:T(128)} %param.31) | copy-start | bytes 772
  137.7 17.5 %all-to-all-start.1 = ((bf16[16,128,128]{2,1,0:T(8,128)(2,1)}), bf16[16,128,128]{2,1,0:T(8,128)(2,1)S(1)}, u32[]{:S(2)}, u32[]{:S(2)}) async-start(bf16[16,128,128]{2,1,0:T(8,128)(2,1)} %copy-done.4), calls=%async_computation.1 | async-start | bytes 1048576 | tf_op jit(solution)/shard_map/all_to_all | solution.py:326
  146.9 11.9 %collective-permute-start.1 = (f32[128]{0:T(128)S(1)}, f32[128]{0:T(128)S(1)}, u32[]{:S(2)}, u32[]{:S(2)}) collective-permute-start(f32[128]{0:T(128)S(1)} %and_select_fusion), channel_id=1, source_target_pairs={{0,64},{64,0},{1,65},{65,1},{2,66},{66,2},{3,67},{67,3},{4,68},{68... | collective-permute-start | bytes 1544 | tf_op jit(solution)/shard_map/ppermute | solution.py:358
  155.2 13.7 %all-to-all-start.3 = ((bf16[16,128,128]{2,1,0:T(8,128)(2,1)}), bf16[16,128,128]{2,1,0:T(8,128)(2,1)S(1)}, u32[]{:S(2)}, u32[]{:S(2)}) async-start(bf16[16,128,128]{2,1,0:T(8,128)(2,1)} %copy-done.3), calls=%async_computation.3 | async-start | bytes 1048576 | tf_op jit(solution)/shard_map/all_to_all | solution.py:326
  160.1 7.2 %collective-permute-start.2 = (f32[128]{0:T(128)S(1)}, f32[128]{0:T(128)S(1)}, u32[]{:S(2)}, u32[]{:S(2)}) collective-permute-start(f32[128]{0:T(128)S(1)} %fusion.4), channel_id=1, source_target_pairs={{0,16},{16,32},{32,48},{48,0},{1,17},{17,33},{33,49},{49,1},{2,18}... | collective-permute-start | bytes 1544 | tf_op jit(solution)/shard_map/ppermute | solution.py:307
  161.7 5.6 %collective-permute-start.3 = (f32[128]{0:T(128)S(1)}, f32[128]{0:T(128)S(1)}, u32[]{:S(2)}, u32[]{:S(2)}) collective-permute-start(f32[128]{0:T(128)S(1)} %fusion.4), channel_id=1, source_target_pairs={{0,32},{16,48},{32,0},{48,16},{1,33},{17,49},{33,1},{49,17},{2,34}... | collective-permute-start | bytes 1544 | tf_op jit(solution)/shard_map/ppermute | solution.py:307
  164.6 3.5 %collective-permute-start.4 = (f32[128]{0:T(128)S(1)}, f32[128]{0:T(128)S(1)}, u32[]{:S(2)}, u32[]{:S(2)}) collective-permute-start(f32[128]{0:T(128)S(1)} %fusion.4), channel_id=1, source_target_pairs={{0,48},{16,0},{32,16},{48,32},{1,49},{17,1},{33,17},{49,33},{2,50}... | collective-permute-start | bytes 1544 | tf_op jit(solution)/shard_map/ppermute | solution.py:307
  180.4 5.3 %collective-permute-start.5 = (f32[128]{0:T(128)S(1)}, f32[128]{0:T(128)S(1)}, u32[]{:S(2)}, u32[]{:S(2)}) collective-permute-start(f32[128]{0:T(128)S(1)} %pad_maximum_fusion), channel_id=1, source_target_pairs={{0,1},{1,2},{2,3},{3,0},{4,5},{5,6},{6,7},{7,4},{8,9},{9,10},{10,1... | collective-permute-start | bytes 1544 | tf_op jit(solution)/shard_map/ppermute | solution.py:307
  181.5 5.0 %collective-permute-start.6 = (f32[128]{0:T(128)S(1)}, f32[128]{0:T(128)S(1)}, u32[]{:S(2)}, u32[]{:S(2)}) collective-permute-start(f32[128]{0:T(128)S(1)} %pad_maximum_fusion), channel_id=1, source_target_pairs={{0,2},{1,3},{2,0},{3,1},{4,6},{5,7},{6,4},{7,5},{8,10},{9,11},{10,... | collective-permute-start | bytes 1544 | tf_op jit(solution)/shard_map/ppermute | solution.py:307
  184.2 3.5 %collective-permute-start.7 = (f32[128]{0:T(128)S(1)}, f32[128]{0:T(128)S(1)}, u32[]{:S(2)}, u32[]{:S(2)}) collective-permute-start(f32[128]{0:T(128)S(1)} %pad_maximum_fusion), channel_id=1, source_target_pairs={{0,3},{1,0},{2,1},{3,2},{4,7},{5,4},{6,5},{7,6},{8,11},{9,8},{10,9... | collective-permute-start | bytes 1544 | tf_op jit(solution)/shard_map/ppermute | solution.py:307
  187.7 5.4 %collective-permute-start.10 = (f32[128]{0:T(128)S(1)}, f32[128]{0:T(128)S(1)}, u32[]{:S(2)}, u32[]{:S(2)}) collective-permute-start(f32[128]{0:T(128)S(1)} %add_select_fusion.1), channel_id=1, source_target_pairs={{0,12},{1,13},{2,14},{3,15},{4,0},{5,1},{6,2},{7,3},{8,4},{9,5},{1... | collective-permute-start | bytes 1544 | tf_op jit(solution)/shard_map/ppermute | solution.py:307
  190.5 4.8 %collective-permute-start.8 = (f32[128]{0:T(128)S(1)}, f32[128]{0:T(128)S(1)}, u32[]{:S(2)}, u32[]{:S(2)}) collective-permute-start(f32[128]{0:T(128)S(1)} %add_select_fusion.1), channel_id=1, source_target_pairs={{0,4},{1,5},{2,6},{3,7},{4,8},{5,9},{6,10},{7,11},{8,12},{9,13},{1... | collective-permute-start | bytes 1544 | tf_op jit(solution)/shard_map/ppermute | solution.py:307
  190.5 5.0 %collective-permute-start.9 = (f32[128]{0:T(128)S(1)}, f32[128]{0:T(128)S(1)}, u32[]{:S(2)}, u32[]{:S(2)}) collective-permute-start(f32[128]{0:T(128)S(1)} %add_select_fusion.1), channel_id=1, source_target_pairs={{0,8},{1,9},{2,10},{3,11},{4,12},{5,13},{6,14},{7,15},{8,0},{9,1},... | collective-permute-start | bytes 1544 | tf_op jit(solution)/shard_map/ppermute | solution.py:307
  193.1 3.8 %collective-permute-start = (f32[2,128,64]{2,1,0:T(8,128)S(1)}, f32[2,128,64]{2,1,0:T(8,128)S(1)}, u32[]{:S(2)}, u32[]{:S(2)}) collective-permute-start(f32[2,128,64]{2,1,0:T(8,128)S(1)} %get-tuple-element.15), channel_id=1, source_target_pairs={{0,64},{64,0},{1,65},{65,1},{2,66},{66,2},{3,67},{67,3},{4,68},{68... | collective-permute-start | bytes 196616 | tf_op jit(solution)/shard_map/ppermute | solution.py:346
  (8 other events, 76.9 us)

commit v2 on v1

--- a/solution.py
+++ b/solution.py
@@ -20,26 +20,30 @@
     return 3.0 * fraction / (1.0 + 2.0 * fraction)
 
 
-def pack_pairs_kernel(q_ref, k_ref, v_ref, tk_ref, tv_ref, out_ref):
+def text_rows(ref, r, cols):
+    return ref[0, :, :, cols].astype(f32)[:, r, :].astype(bf16)
+
+
+def pack_pairs_kernel(r, q_ref, k_ref, v_ref, tk_ref, tv_ref, out_ref):
     tok = q_ref.shape[2]
-    txt = tk_ref.shape[2]
+    txt = tk_ref.shape[1]
     for i in range(out_ref.shape[0]):
         cols = slice(i * LANES, (i + 1) * LANES)
         out_ref[i, 0:tok, :] = q_ref[0, 0, :, cols]
         out_ref[i, tok : 2 * tok, :] = k_ref[0, 0, :, cols]
         out_ref[i, 2 * tok : 3 * tok, :] = v_ref[0, 0, :, cols]
-        out_ref[i, 3 * tok : 3 * tok + txt, :] = tk_ref[0, 0, :, cols]
-        out_ref[i, 3 * tok + txt : 3 * tok + 2 * txt, :] = tv_ref[0, 0, :, cols]
+        out_ref[i, 3 * tok : 3 * tok + txt, :] = text_rows(tk_ref, r, cols)
+        out_ref[i, 3 * tok + txt : 3 * tok + 2 * txt, :] = text_rows(tv_ref, r, cols)
 
 
 def pack_pairs(r, q, k, v, tk, tv, shards):
-    tok, txt = q.shape[2], tk.shape[2]
+    tok, txt = q.shape[2], tk.shape[1]
     rows = 3 * tok + 2 * txt
     per = 4
     img = pl.BlockSpec((1, 1, tok, per * LANES), lambda j: (0, r, 0, j))
-    text = pl.BlockSpec((1, 1, txt, per * LANES), lambda j: (0, r, 0, j))
+    text = pl.BlockSpec((1, txt, 2, per * LANES), lambda j: (0, 0, 0, j))
     return pl.pallas_call(
-        pack_pairs_kernel,
+        functools.partial(pack_pairs_kernel, r),
         grid=(shards // per,),
         in_specs=[img, img, img, text, text],
         out_specs=pl.BlockSpec((per, rows, LANES), lambda j: (j, 0, 0)),
@@ -52,7 +56,7 @@
 def pack_single_kernel(n_pairs, q_ref, k_ref, v_ref, tk_ref, tv_ref, out_ref):
     j = pl.program_id(0)
     tok = q_ref.shape[2]
-    txt = tk_ref.shape[2]
+    txt = tk_ref.shape[1]
     half = tok // 2
     hd = LANES // 2
 
@@ -70,7 +74,7 @@
                         folded = jnp.concatenate([top[:, hd:], low[:, hd:]], axis=1)
                     out_ref[d, n * half : (n + 1) * half, :] = folded
                 for n, ref in enumerate((tk_ref, tv_ref)):
-                    x = ref[0, r][:, h * hd : (h + 1) * hd]
+                    x = text_rows(ref, r, slice(0, LANES))[:, h * hd : (h + 1) * hd]
                     base = 3 * half + n * txt
                     out_ref[d, base : base + txt, :] = jnp.concatenate([x, x], axis=1)
 
@@ -80,12 +84,12 @@
 
 
 def pack_single(q, k, v, tk, tv, shards):
-    tok, txt = q.shape[2], tk.shape[2]
+    tok, txt = q.shape[2], tk.shape[1]
     n_pairs = q.shape[3] // LANES - shards
     rows = 3 * (tok // 2) + 2 * txt
     last = n_pairs - 1
     img = pl.BlockSpec((1, 2, tok, LANES), lambda j: (0, 0, 0, shards + jnp.minimum(j, last)))
-    text = pl.BlockSpec((1, 2, txt, LANES), lambda j: (0, 0, 0, shards + jnp.minimum(j, last)))
+    text = pl.BlockSpec((1, txt, 2, LANES), lambda j: (0, 0, 0, shards + jnp.minimum(j, last)))
     return pl.pallas_call(
         functools.partial(pack_single_kernel, n_pairs),
         grid=(shards // 4,),
@@ -97,7 +101,9 @@
     )(q, k, v, tk, tv)
 
 
-def attend_kernel(folded, tok, txt, len_ref, r_ref, o_ref, top_ref, k2, vt, top):
+def attend_kernel(which, carried, folded, tok, txt, len_ref, r_ref, *refs):
+    c_ref = refs[0] if carried else None
+    o_ref, top_ref, k2, vt, top = refs[-5:]
     shards = r_ref.shape[0]
     hd = LANES // 2
     rows = tok // 2 if folded else tok
@@ -105,7 +111,7 @@
     slot = 16
     n_txt = shards * slot
     t = pl.program_id(0)
-    length = len_ref[0]
+    length = len_ref[which]
 
     @pl.when(t == 0)
     def _prep():
@@ -174,7 +180,9 @@
         outs.append(o[:hd] / o[hd : hd + 1])
         top[h : h + 1, :] = jnp.maximum(top[h : h + 1, :], m)
     out = jnp.concatenate(outs, axis=0).T.astype(bf16)
-    o_ref[...] = out.reshape(per, rows, LANES)
+    o_ref[:, 0:rows, :] = out.reshape(per, rows, LANES)
+    if carried:
+        o_ref[:, rows:, :] = c_ref[...]
 
     @pl.when(t == pl.num_programs(0) - 1)
     def _fin():
@@ -182,25 +190,28 @@
         top_ref[...] = jnp.broadcast_to(best, top_ref.shape)
 
 
-def attend(received, length, tok, txt, folded):
+def attend(received, lengths, which, tok, txt, folded, carry=None):
     shards, total, _ = received.shape
     rows = tok // 2 if folded else tok
     n_keys = shards * (tok + 16)
     per = QT // rows
     heads = 1 if folded else 2
+    extra = [] if carry is None else [carry]
+    out_rows = rows + sum(x.shape[1] for x in extra)
     return pl.pallas_call(
-        functools.partial(attend_kernel, folded, tok, txt),
+        functools.partial(attend_kernel, which, carry is not None, folded, tok, txt),
         grid=(shards // per,),
         in_specs=[
             pl.BlockSpec(memory_space=pltpu.SMEM),
             pl.BlockSpec((shards, total, LANES), lambda t: (0, 0, 0)),
-        ],
+        ]
+        + [pl.BlockSpec((per,) + x.shape[1:], lambda t: (t, 0, 0)) for x in extra],
         out_specs=[
-            pl.BlockSpec((per, rows, LANES), lambda t: (t, 0, 0)),
+            pl.BlockSpec((per, out_rows, LANES), lambda t: (t, 0, 0)),
             pl.BlockSpec((8, LANES), lambda t: (0, 0)),
         ],
         out_shape=[
-            jax.ShapeDtypeStruct((shards, rows, LANES), bf16),
+            jax.ShapeDtypeStruct((shards, out_rows, LANES), bf16),
             jax.ShapeDtypeStruct((8, LANES), f32),
         ],
         scratch_shapes=[
@@ -215,14 +226,14 @@
             transcendentals=heads * shards * tok * n_keys,
         ),
         name="attend_single" if folded else "attend_pair",
-    )(length, received)
+    )(lengths, received, *extra)
 
 
 def finish_kernel(
-    n_pairs, half_ref, a_ref, b_ref, c_ref, hid_ref, gate_ref, mod_ref, ob_ref, fw_ref, fb_ref, w_hbm,
+    n_pairs, half_ref, a_ref, b_ref, hid_ref, gate_ref, mod_ref, ob_ref, fw_ref, w_hbm,
     pred_ref, sq_ref, att, w, acc, sem,
 ):
-    shards, tok, _ = a_ref.shape
+    shards, tok, _ = b_ref.shape
     width = w.shape[0]
     hd = LANES // 2
     half = tok // 2
@@ -234,12 +245,12 @@
     for copy in copies:
         copy.start()
     for d in range(shards):
-        att[0:tok, d * LANES : (d + 1) * LANES] = a_ref[d]
+        att[0:tok, d * LANES : (d + 1) * LANES] = a_ref[d, 0:tok]
         att[tok:, d * LANES : (d + 1) * LANES] = b_ref[d]
     for j in range(n_pairs):
         for r in range(2):
-            x0 = c_ref[4 * j + 2 * r]
-            x1 = c_ref[4 * j + 2 * r + 1]
+            x0 = a_ref[4 * j + 2 * r, tok:]
+            x1 = a_ref[4 * j + 2 * r + 1, tok:]
             cols = slice((shards + j) * LANES, (shards + j + 1) * LANES)
             att[r * tok : r * tok + half, cols] = jnp.concatenate([x0[:, :hd], x1[:, :hd]], axis=1)
             att[r * tok + half : (r + 1) * tok, cols] = jnp.concatenate([x0[:, hd:], x1[:, hd:]], axis=1)
@@ -270,22 +281,24 @@
 
         total = lax.fori_loop(0, tok // step, body, jnp.zeros((step, 1), f32))
         sq_ref[r : r + 1, :] = jnp.broadcast_to(jnp.sum(total, axis=0, keepdims=True), (1, LANES))
-        pred = jnp.dot(att[r * tok : (r + 1) * tok, :], fw_ref[...], preferred_element_type=f32)
-        pred_ref[r] = half_ref[r] * (pred + fb_ref[...])
-
-
-def finish(half_weight, ra, rb, rc, hidden_in, gate, mod, out_bias, final_weight, final_bias, out_weight):
-    shards, tok, _ = ra.shape
+        pred = lax.dot_general(
+            fw_ref[...], att[r * tok : (r + 1) * tok, :], (((1,), (1,)), ((), ())), preferred_element_type=f32
+        )
+        pred_ref[r] = half_ref[r] * pred
+
+
+def finish(half_weight, ra, rb, hidden_in, gate, mod, out_bias, final_weight, out_weight):
+    shards, tok, _ = rb.shape
     width = out_weight.shape[0]
-    c_out = final_weight.shape[1]
+    c_out = final_weight.shape[0]
     n_pairs = width // LANES - shards
     vmem = pl.BlockSpec(memory_space=pltpu.VMEM)
     return pl.pallas_call(
         functools.partial(finish_kernel, n_pairs),
-        in_specs=[pl.BlockSpec(memory_space=pltpu.SMEM)] + [vmem] * 9 + [pl.BlockSpec(memory_space=pl.ANY)],
+        in_specs=[pl.BlockSpec(memory_space=pltpu.SMEM)] + [vmem] * 7 + [pl.BlockSpec(memory_space=pl.ANY)],
         out_specs=[vmem, vmem],
         out_shape=[
-            jax.ShapeDtypeStruct((2, tok, c_out), f32),
+            jax.ShapeDtypeStruct((2, c_out, tok), f32),
             jax.ShapeDtypeStruct((8, LANES), f32),
         ],
         scratch_shapes=[
@@ -299,7 +312,7 @@
             flops=4 * tok * width * (width + c_out), bytes_accessed=2 * width * width, transcendentals=0
         ),
         name="finish",
-    )(half_weight, ra, rb, rc, hidden_in, gate, mod, out_bias, final_weight, final_bias, out_weight)
+    )(half_weight, ra, rb, hidden_in, gate, mod, out_bias, final_weight, out_weight)
 
 
 def ring_stage(x, axis, size, move, combine):
@@ -320,32 +333,37 @@
     image_rows = tok * shards
     per_shard = (head_count + shards - 1) // shards
 
-    streams = (img_query, img_key, img_value, txt_key, txt_value)
+    text = [x.transpose(0, 2, 1, 3) for x in (txt_key, txt_value)]
+    streams = (img_query, img_key, img_value, *text)
 
     def swap(x):
         return lax.all_to_all(x, "seq", split_axis=0, concat_axis=0, tiled=True)
 
-    lengths = text_len[0]
-    length_c = jnp.where((position % 4) // 2 == 0, lengths[0], lengths[1])
-
+    length_c = jnp.where((position % 4) // 2 == 0, text_len[0, 0], text_len[0, 1])
+    lengths = jnp.stack([text_len[0, 0], text_len[0, 1], length_c])
+    half_weight = jnp.where(lax.axis_index("cfg") == 0, guidance, 1.0 - guidance)
+    lengths, half_weight, first = lax.optimization_barrier(
+        (lengths, half_weight, pack_single(*streams, shards))
+    )
+
+    in_c = swap(first)
     in_a = swap(pack_pairs(0, *streams, shards))
-    in_b = swap(pack_pairs(1, *streams, shards))
-    in_c = swap(pack_single(*streams, shards))
-    out_a, top_a = attend(in_a, lengths[0:1], tok, txt, False)
+    out_c, top_c = attend(in_c, lengths, 2, tok, txt, True)
+    second, out_c = lax.optimization_barrier((pack_pairs(1, *streams, shards), out_c))
+    in_b = swap(second)
+    out_a, top_a = attend(in_a, lengths, 0, tok, txt, False, out_c)
     back_a = swap(out_a)
-    out_b, top_b = attend(in_b, lengths[1:2], tok, txt, False)
+    out_b, top_b = attend(in_b, lengths, 1, tok, txt, False)
     back_b = swap(out_b)
-    out_c, top_c = attend(in_c, length_c[None], tok, txt, True)
-    back_c = swap(out_c)
-
-    half_weight = jnp.where(lax.axis_index("cfg") == 0, guidance, 1.0 - guidance)
+
     pred, squares = finish(
-        half_weight, back_a, back_b, back_c, hidden_in, attn_gate, final_mod,
-        out_bias[None], final_weight, final_bias[None], out_weight,
+        half_weight, back_a, back_b, hidden_in, attn_gate, final_mod,
+        out_bias[None], final_weight.T, out_weight,
     )
-    velocity = pred + lax.ppermute(pred, "cfg", [(0, 1), (1, 0)])
+    velocity = pred + lax.ppermute(pred, "cfg", [(0, 1), (1, 0)]) + final_bias[None, :, None]
     step_size = (sigma_of(timesteps - 1) - sigma_of(timesteps))[:, None, None]
-    latent_next = latent + step_size * velocity
+    latent_next = latent.transpose(0, 2, 1) + step_size * velocity
+    velocity, latent_next = velocity.transpose(0, 2, 1), latent_next.transpose(0, 2, 1)
 
     lane = jnp.arange(LANES, dtype=jnp.int32)
     pair_top = jnp.maximum(top_a[0:2, 0], top_b[0:2, 0])

time: 199 us -> 179 us (0.90)
  waiting for transfers between devices: 45.7 us -> 33.2 us
  starting transfers between devices: 49.8 us -> 41.8 us
  local copies, waits for them, and re-layouts: 11.5 us -> 6.44 us
  other arithmetic: 4.27 us -> 6.94 us
  Pallas kernels: 83.4 us -> 85.7 us
    all_to_all x6 -> x5, waiting for transfers between devices: 40.4 us -> 21.1 us  [swap(): return lax.all_to_all(x, 'seq', split_axis=0, concat_axis=0, tiled=True)]
    ppermute x9, waiting for transfers between devices: 5.29 us -> 12.1 us  [ring_stage(): others = [lax.ppermute(x, axis, p) for p in pairs]]
    unnamed x36 -> x22, local copies, waits for them, and re-layouts: 9.71 us -> 3.96 us
    ppermute x9, starting transfers between devices: 16.2 us -> 11.9 us  [ring_stage(): others = [lax.ppermute(x, axis, p) for p in pairs]]
    all_to_all x6 -> x5, starting transfers between devices: 33.4 us -> 29.7 us  [swap(): return lax.all_to_all(x, 'seq', split_axis=0, concat_axis=0, tiled=True)]
  transfers between devices with their start and end apart: 17 -> 16, of which waited for: 9 -> 10; matrix products, arithmetic and copies ran while one was open for 4% -> 3% of each run, Pallas kernels for 35% -> 40%
where the time goes in v2:
time: 179 us; the launch traced here: 178 us
  Pallas kernels  85.7 us (48%)
  starting transfers between devices  41.8 us (23%)
  waiting for transfers between devices  33.2 us (19%)
  other arithmetic  6.94 us (4%)
  local copies, waits for them, and re-layouts  6.44 us (4%)
  between operations  3.5 us (2%)
    pallas_call x3, Pallas kernels, attend(): pl.pallas_call(functools.partial(attend_kernel, which, carry is not None,...  63.5 us
    all_to_all x5, starting transfers between devices, swap(): return lax.all_to_all(x, 'seq', split_axis=0, concat_axis=0, tiled=True)  29.7 us
    all_to_all x5, waiting for transfers between devices, swap(): return lax.all_to_all(x, 'seq', split_axis=0, concat_axis=0, tiled=True)  21.1 us
    ppermute x9, waiting for transfers between devices, ring_stage(): others = [lax.ppermute(x, axis, p) for p in pairs]  12.1 us
    ppermute x9, starting transfers between devices, ring_stage(): others = [lax.ppermute(x, axis, p) for p in pairs]  11.9 us
    pallas_call x1, Pallas kernels, finish(): pl.pallas_call(functools.partial(finish_kernel, n_pairs), in_specs=[pl.Bl...  11.5 us
    pallas_call x2, Pallas kernels, pack_pairs(): pl.pallas_call(functools.partial(pack_pairs_kernel, r), grid=(shards // p...  7.68 us
    unnamed x22, local copies, waits for them, and re-layouts  3.96 us
  transfers between devices with their start and end apart: 16, of which 10 were waited for; matrix products, arithmetic and copies ran while one was open for 3% of the time, Pallas kernels for 40%

profile of v2, /device:TPU:0, one launch (start us, length us, event | category | flops | bytes accessed | tf_op | source)
XLA Modules:
  0.0 177.5 jit_solution(5740842324107871149)
XLA Ops:
  3.9 1.4 pad_add_fusion.len_ref
  5.3 3.0 %pack_single.1 = bf16[16,212,128]{2,1,0:T(8,128)(2,1)} custom-call(bf16[1,2,128,2432]{3,2,1,0:T(8,128)(2,1)} %q_ref.5, bf16[1,2,128,2432]{3,2,1,0:T(8,128)(2,1)} %k_ref.5, bf16[1,2,128,2432]{3,2,1,0:T(8,128)(2,1)} %v_ref.5, bf16[1,10,2,2432]{3,2,1,0:T(2,128)(2,1)} %bitcast.24, bf16[1,10,2,2432]{3,2,1,0:T(2,128)(2,1)} %bitcast.27), custom_call_target="tpu_custom_call" | custom-call | bytes 1736704 | tf_op jit(solution)/shard_map/pack_single/pallas_call | solution.py:93
  8.3 8.0 %all-to-all-start.1 = ((bf16[16,212,128]{2,1,0:T(8,128)(2,1)}), bf16[16,212,128]{2,1,0:T(8,128)(2,1)S(1)}, u32[]{:S(2)}, u32[]{:S(2)}) async-start(bf16[16,212,128]{2,1,0:T(8,128)(2,1)} %pack_single.1), calls=%async_computation.1 | async-start | bytes 1769472 | tf_op jit(solution)/shard_map/all_to_all | solution.py:340
  16.3 3.9 %pack_pairs.2 = bf16[16,404,128]{2,1,0:T(8,128)(2,1)} custom-call(bf16[1,2,128,2432]{3,2,1,0:T(8,128)(2,1)} %q_ref.5, bf16[1,2,128,2432]{3,2,1,0:T(8,128)(2,1)} %k_ref.5, bf16[1,2,128,2432]{3,2,1,0:T(8,128)(2,1)} %v_ref.5, bf16[1,10,2,2432]{3,2,1,0:T(2,128)(2,1)} %bitcast.25, bf16[1,10,2,2432]{3,2,1,0:T(2,128)(2,1)} %bitcast.28), custom_call_target="tpu_custom_call" | custom-call | bytes 3309568 | tf_op jit(solution)/shard_map/pack_pairs/pallas_call | solution.py:45
  20.2 11.8 %all-to-all-done.1.r_ref = bf16[16,212,128]{2,1,0:T(8,128)(2,1)S(1)} async-done(((bf16[16,212,128]{2,1,0:T(8,128)(2,1)}), bf16[16,212,128]{2,1,0:T(8,128)(2,1)S(1)}, u32[]{:S(2)}, u32[]{:S(2)}) %all-to-all-start.1) | async-done | bytes 868384 | tf_op jit(solution)/shard_map/all_to_all | solution.py:340
  32.0 3.7 %all-to-all-start = ((bf16[16,404,128]{2,1,0:T(8,128)(2,1)}), bf16[16,404,128]{2,1,0:T(8,128)(2,1)S(1)}, u32[]{:S(2)}, u32[]{:S(2)}) async-start(bf16[16,404,128]{2,1,0:T(8,128)(2,1)} %pack_pairs.2), calls=%async_computation | async-start | bytes 3342336 | tf_op jit(solution)/shard_map/all_to_all | solution.py:340
  35.7 3.8 %pack_pairs.3 = bf16[16,404,128]{2,1,0:T(8,128)(2,1)} custom-call(bf16[1,2,128,2432]{3,2,1,0:T(8,128)(2,1)} %q_ref.5, bf16[1,2,128,2432]{3,2,1,0:T(8,128)(2,1)} %k_ref.5, bf16[1,2,128,2432]{3,2,1,0:T(8,128)(2,1)} %v_ref.5, bf16[1,10,2,2432]{3,2,1,0:T(2,128)(2,1)} %bitcast.26, bf16[1,10,2,2432]{3,2,1,0:T(2,128)(2,1)} %bitcast.29), custom_call_target="tpu_custom_call" | custom-call | bytes 3309568 | tf_op jit(solution)/shard_map/pack_pairs/pallas_call | solution.py:45
  39.5 12.7 %attend_single.1 = (bf16[16,64,128]{2,1,0:T(8,128)(2,1)S(1)}, f32[8,128]{1,0:T(8,128)S(1)}) custom-call(s32[3]{0:T(128)S(1)} %pad_add_fusion.len_ref, bf16[16,212,128]{2,1,0:T(8,128)(2,1)S(1)} %all-to-all-done.1.r_ref), custom_call_target="tpu_custom_call" | custom-call | flops 2415919104 | bytes 1736704 | tf_op jit(solution)/shard_map/attend_single/pallas_call | solution.py:201
  52.3 6.9 %all-to-all-done.r_ref = bf16[16,404,128]{2,1,0:T(8,128)(2,1)S(1)} async-done(((bf16[16,404,128]{2,1,0:T(8,128)(2,1)}), bf16[16,404,128]{2,1,0:T(8,128)(2,1)S(1)}, u32[]{:S(2)}, u32[]{:S(2)}) %all-to-all-start) | async-done | bytes 1654816 | tf_op jit(solution)/shard_map/all_to_all | solution.py:340
  60.3 3.7 %all-to-all-start.3 = ((bf16[16,404,128]{2,1,0:T(8,128)(2,1)}), bf16[16,404,128]{2,1,0:T(8,128)(2,1)S(1)}, u32[]{:S(2)}, u32[]{:S(2)}) async-start(bf16[16,404,128]{2,1,0:T(8,128)(2,1)} %pack_pairs.3), calls=%async_computation.3 | async-start | bytes 3342336 | tf_op jit(solution)/shard_map/all_to_all | solution.py:340
  65.9 1.4 copy-done.1
  67.3 25.3 %attend_pair.2 = (bf16[16,192,128]{2,1,0:T(8,128)(2,1)}, f32[8,128]{1,0:T(8,128)S(1)}) custom-call(s32[3]{0:T(128)S(1)} %pad_add_fusion.len_ref, bf16[16,404,128]{2,1,0:T(8,128)(2,1)S(1)} %copy-done.1, bf16[16,64,128]{2,1,0:T(8,128)(2,1)S(1)} %get-tuple-element.21.refs_0_), custom_call_target="tpu_custom_call" | custom-call | flops 4831838208 | bytes 3309568 | tf_op jit(solution)/shard_map/attend_pair/pallas_call | solution.py:201
  92.7 7.1 %all-to-all-start.2 = ((bf16[16,192,128]{2,1,0:T(8,128)(2,1)}), bf16[16,192,128]{2,1,0:T(8,128)(2,1)S(1)}, u32[]{:S(2)}, u32[]{:S(2)}) async-start(bf16[16,192,128]{2,1,0:T(8,128)(2,1)} %get-tuple-element.22), calls=%async_computation.2 | async-start | bytes 1572864 | tf_op jit(solution)/shard_map/all_to_all | solution.py:340
  99.9 25.4 %attend_pair.3 = (bf16[16,128,128]{2,1,0:T(8,128)(2,1)}, f32[8,128]{1,0:T(8,128)S(1)}) custom-call(s32[3]{0:T(128)S(1)} %pad_add_fusion.len_ref, bf16[16,404,128]{2,1,0:T(8,128)(2,1)S(1)} %all-to-all-done.3.r_ref), custom_call_target="tpu_custom_call" | custom-call | flops 4831838208 | bytes 3309568 | tf_op jit(solution)/shard_map/attend_pair/pallas_call | solution.py:201
  127.2 7.2 %all-to-all-start.4 = ((bf16[16,128,128]{2,1,0:T(8,128)(2,1)}), bf16[16,128,128]{2,1,0:T(8,128)(2,1)S(1)}, u32[]{:S(2)}, u32[]{:S(2)}) async-start(bf16[16,128,128]{2,1,0:T(8,128)(2,1)} %get-tuple-element.24), calls=%async_computation.4 | async-start | bytes 1048576 | tf_op jit(solution)/shard_map/all_to_all | solution.py:340
  135.8 3.1 %collective-permute-start.4 = (f32[128]{0:T(128)S(1)}, f32[128]{0:T(128)S(1)}, u32[]{:S(2)}, u32[]{:S(2)}) collective-permute-start(f32[128]{0:T(128)S(1)} %fusion.6), channel_id=1, source_target_pairs={{0,48},{16,0},{32,16},{48,32},{1,49},{17,1},{33,17},{49,33},{2,50}... | collective-permute-start | bytes 1544 | tf_op jit(solution)/shard_map/ppermute | solution.py:320
  140.5 3.4 %collective-permute-done.3 = f32[128]{0:T(128)S(1)} collective-permute-done((f32[128]{0:T(128)S(1)}, f32[128]{0:T(128)S(1)}, u32[]{:S(2)}, u32[]{:S(2)}) %collective-permute-start.3) | collective-permute-done | bytes 544 | tf_op jit(solution)/shard_map/ppermute | solution.py:320
  144.2 2.4 %all-to-all-done.4.b_ref = bf16[16,128,128]{2,1,0:T(8,128)(2,1)S(1)} async-done(((bf16[16,128,128]{2,1,0:T(8,128)(2,1)}), bf16[16,128,128]{2,1,0:T(8,128)(2,1)S(1)}, u32[]{:S(2)}, u32[]{:S(2)}) %all-to-all-start.4) | async-done | bytes 524320 | tf_op jit(solution)/shard_map/all_to_all | solution.py:340
  147.9 11.5 %finish.1 = (f32[2,64,128]{2,1,0:T(8,128)S(1)}, f32[8,128]{1,0:T(8,128)S(1)}) custom-call(f32[2]{0:T(128)S(1)} %broadcast_select_fusion.half_ref, bf16[16,192,128]{2,1,0:T(8,128)(2,1)S(1)} %all-to-all-done.2.a_ref, bf16[16,128,128]{2,1,0:T(8,128)(2,1)S(1)} %all-to-all-done.4.b_ref, bf16[1,2,128,2432]{3,2,1,0:T(8,128)(2,1)S(1)} %copy-done.2, ...), custom_call_target="tpu_custom_call" | custom-call | flops 3107979264 | bytes 11829248 | tf_op jit(solution)/shard_map/finish/pallas_call | solution.py:296
  160.7 2.2 %collective-permute-start.7 = (f32[128]{0:T(128)S(1)}, f32[128]{0:T(128)S(1)}, u32[]{:S(2)}, u32[]{:S(2)}) collective-permute-start(f32[128]{0:T(128)S(1)} %pad_maximum_fusion), channel_id=1, source_target_pairs={{0,3},{1,0},{2,1},{3,2},{4,7},{5,4},{6,5},{7,6},{8,11},{9,8},{10,9... | collective-permute-start | bytes 1544 | tf_op jit(solution)/shard_map/ppermute | solution.py:320
  162.9 1.8 %collective-permute-done.6 = f32[128]{0:T(128)S(1)} collective-permute-done((f32[128]{0:T(128)S(1)}, f32[128]{0:T(128)S(1)}, u32[]{:S(2)}, u32[]{:S(2)}) %collective-permute-start.6) | collective-permute-done | bytes 544 | tf_op jit(solution)/shard_map/ppermute | solution.py:320
  164.7 2.9 %collective-permute-done.5 = f32[128]{0:T(128)S(1)} collective-permute-done((f32[128]{0:T(128)S(1)}, f32[128]{0:T(128)S(1)}, u32[]{:S(2)}, u32[]{:S(2)}) %collective-permute-start.5) | collective-permute-done | bytes 544 | tf_op jit(solution)/shard_map/ppermute | solution.py:320
  167.6 2.0 %collective-permute-start.9 = (f32[128]{0:T(128)S(1)}, f32[128]{0:T(128)S(1)}, u32[]{:S(2)}, u32[]{:S(2)}) collective-permute-start(f32[128]{0:T(128)S(1)} %add_select_fusion.1), channel_id=1, source_target_pairs={{0,8},{1,9},{2,10},{3,11},{4,12},{5,13},{6,14},{7,15},{8,0},{9,1},... | collective-permute-start | bytes 1544 | tf_op jit(solution)/shard_map/ppermute | solution.py:320
  173.1 2.4 %collective-permute-done.8 = f32[128]{0:T(128)S(1)} collective-permute-done((f32[128]{0:T(128)S(1)}, f32[128]{0:T(128)S(1)}, u32[]{:S(2)}, u32[]{:S(2)}) %collective-permute-start.8) | collective-permute-done | bytes 544 | tf_op jit(solution)/shard_map/ppermute | solution.py:320
  (58 shorter events, 17.0 us)
Async XLA Ops:
  8.3 23.6 %all-to-all-start.1 = ((bf16[16,212,128]{2,1,0:T(8,128)(2,1)}), bf16[16,212,128]{2,1,0:T(8,128)(2,1)S(1)}, u32[]{:S(2)}, u32[]{:S(2)}) async-start(bf16[16,212,128]{2,1,0:T(8,128)(2,1)} %pack_single.1), calls=%async_computation.1 | async-start | bytes 1769472 | tf_op jit(solution)/shard_map/all_to_all | solution.py:340
  32.0 27.2 %all-to-all-start = ((bf16[16,404,128]{2,1,0:T(8,128)(2,1)}), bf16[16,404,128]{2,1,0:T(8,128)(2,1)S(1)}, u32[]{:S(2)}, u32[]{:S(2)}) async-start(bf16[16,404,128]{2,1,0:T(8,128)(2,1)} %pack_pairs.2), calls=%async_computation | async-start | bytes 3342336 | tf_op jit(solution)/shard_map/all_to_all | solution.py:340
  60.3 32.4 %all-to-all-start.3 = ((bf16[16,404,128]{2,1,0:T(8,128)(2,1)}), bf16[16,404,128]{2,1,0:T(8,128)(2,1)S(1)}, u32[]{:S(2)}, u32[]{:S(2)}) async-start(bf16[16,404,128]{2,1,0:T(8,128)(2,1)} %pack_pairs.3), calls=%async_computation.3 | async-start | bytes 3342336 | tf_op jit(solution)/shard_map/all_to_all | solution.py:340
  92.7 34.5 %all-to-all-start.2 = ((bf16[16,192,128]{2,1,0:T(8,128)(2,1)}), bf16[16,192,128]{2,1,0:T(8,128)(2,1)S(1)}, u32[]{:S(2)}, u32[]{:S(2)}) async-start(bf16[16,192,128]{2,1,0:T(8,128)(2,1)} %get-tuple-element.22), calls=%async_computation.2 | async-start | bytes 1572864 | tf_op jit(solution)/shard_map/all_to_all | solution.py:340
  99.8 40.6 %copy-start.10 = (s32[2]{0:T(128)S(1)}, s32[2]{0:T(128)}, u32[]{:S(2)}) copy-start(s32[2]{0:T(128)} %param.32) | copy-start | bytes 28
  99.8 40.6 %copy-start.7 = (f32[2432]{0:T(1024)S(1)}, f32[2432]{0:T(1024)}, u32[]{:S(2)}) copy-start(f32[2432]{0:T(1024)} %param.27) | copy-start | bytes 29188
  99.9 46.8 %copy-start.3 = (bf16[2432,64]{0,1:T(8,128)(2,1)S(1)}, bf16[2432,64]{0,1:T(8,128)(2,1)}, u32[]{:S(2)}) copy-start(bf16[2432,64]{0,1:T(8,128)(2,1)} %param.30) | copy-start | bytes 933892
  99.9 46.8 %copy-start.4 = (f32[1,2,2,2432]{3,2,1,0:T(2,128)S(1)}, f32[1,2,2,2432]{3,2,1,0:T(2,128)}, u32[]{:S(2)}) copy-start(f32[1,2,2,2432]{3,2,1,0:T(2,128)} %mod_ref.1) | copy-start | bytes 116740
  99.9 46.7 %copy-start.5 = (f32[1,2,2432]{2,1,0:T(2,128)S(1)}, f32[1,2,2432]{2,1,0:T(2,128)}, u32[]{:S(2)}) copy-start(f32[1,2,2432]{2,1,0:T(2,128)} %gate_ref.1) | copy-start | bytes 58372
  127.1 7.3 %collective-permute-start.1 = (f32[128]{0:T(128)S(1)}, f32[128]{0:T(128)S(1)}, u32[]{:S(2)}, u32[]{:S(2)}) collective-permute-start(f32[128]{0:T(128)S(1)} %and_select_fusion), channel_id=1, source_target_pairs={{0,64},{64,0},{1,65},{65,1},{2,66},{66,2},{3,67},{67,3},{4,68},{68... | collective-permute-start | bytes 1544 | tf_op jit(solution)/shard_map/ppermute | solution.py:376
  127.2 19.4 %all-to-all-start.4 = ((bf16[16,128,128]{2,1,0:T(8,128)(2,1)}), bf16[16,128,128]{2,1,0:T(8,128)(2,1)S(1)}, u32[]{:S(2)}, u32[]{:S(2)}) async-start(bf16[16,128,128]{2,1,0:T(8,128)(2,1)} %get-tuple-element.24), calls=%async_computation.4 | async-start | bytes 1048576 | tf_op jit(solution)/shard_map/all_to_all | solution.py:340
  135.8 4.7 %collective-permute-start.4 = (f32[128]{0:T(128)S(1)}, f32[128]{0:T(128)S(1)}, u32[]{:S(2)}, u32[]{:S(2)}) collective-permute-start(f32[128]{0:T(128)S(1)} %fusion.6), channel_id=1, source_target_pairs={{0,48},{16,0},{32,16},{48,32},{1,49},{17,1},{33,17},{49,33},{2,50}... | collective-permute-start | bytes 1544 | tf_op jit(solution)/shard_map/ppermute | solution.py:320
  138.8 5.0 %collective-permute-start.3 = (f32[128]{0:T(128)S(1)}, f32[128]{0:T(128)S(1)}, u32[]{:S(2)}, u32[]{:S(2)}) collective-permute-start(f32[128]{0:T(128)S(1)} %fusion.6), channel_id=1, source_target_pairs={{0,32},{16,48},{32,0},{48,16},{1,33},{17,49},{33,1},{49,17},{2,34}... | collective-permute-start | bytes 1544 | tf_op jit(solution)/shard_map/ppermute | solution.py:320
  139.5 4.8 %collective-permute-start.2 = (f32[128]{0:T(128)S(1)}, f32[128]{0:T(128)S(1)}, u32[]{:S(2)}, u32[]{:S(2)}) collective-permute-start(f32[128]{0:T(128)S(1)} %fusion.6), channel_id=1, source_target_pairs={{0,16},{16,32},{32,48},{48,0},{1,17},{17,33},{33,49},{49,1},{2,18}... | collective-permute-start | bytes 1544 | tf_op jit(solution)/shard_map/ppermute | solution.py:320
  147.9 23.7 %copy-start.9 = (s32[38]{0:T(128)S(1)}, s32[38]{0:T(128)}, u32[]{:S(2)}) copy-start(s32[38]{0:T(128)} %param.25) | copy-start | bytes 460
  147.9 28.9 %copy-start.6 = (f32[2,128,64]{1,2,0:T(8,128)S(1)}, f32[2,128,64]{1,2,0:T(8,128)}, u32[]{:S(2)}) copy-start(f32[2,128,64]{1,2,0:T(8,128)} %param.17) | copy-start | bytes 196612
  147.9 28.9 %copy-start.8 = (f32[64]{0:T(128)S(1)}, f32[64]{0:T(128)}, u32[]{:S(2)}) copy-start(f32[64]{0:T(128)} %param.31) | copy-start | bytes 772
  159.6 5.1 %collective-permute-start.6 = (f32[128]{0:T(128)S(1)}, f32[128]{0:T(128)S(1)}, u32[]{:S(2)}, u32[]{:S(2)}) collective-permute-start(f32[128]{0:T(128)S(1)} %pad_maximum_fusion), channel_id=1, source_target_pairs={{0,2},{1,3},{2,0},{3,1},{4,6},{5,7},{6,4},{7,5},{8,10},{9,11},{10,... | collective-permute-start | bytes 1544 | tf_op jit(solution)/shard_map/ppermute | solution.py:320
  160.7 4.0 %collective-permute-start.7 = (f32[128]{0:T(128)S(1)}, f32[128]{0:T(128)S(1)}, u32[]{:S(2)}, u32[]{:S(2)}) collective-permute-start(f32[128]{0:T(128)S(1)} %pad_maximum_fusion), channel_id=1, source_target_pairs={{0,3},{1,0},{2,1},{3,2},{4,7},{5,4},{6,5},{7,6},{8,11},{9,8},{10,9... | collective-permute-start | bytes 1544 | tf_op jit(solution)/shard_map/ppermute | solution.py:320
  162.9 4.8 %collective-permute-start.5 = (f32[128]{0:T(128)S(1)}, f32[128]{0:T(128)S(1)}, u32[]{:S(2)}, u32[]{:S(2)}) collective-permute-start(f32[128]{0:T(128)S(1)} %pad_maximum_fusion), channel_id=1, source_target_pairs={{0,1},{1,2},{2,3},{3,0},{4,5},{5,6},{6,7},{7,4},{8,9},{9,10},{10,1... | collective-permute-start | bytes 1544 | tf_op jit(solution)/shard_map/ppermute | solution.py:320
  167.6 5.0 %collective-permute-start.9 = (f32[128]{0:T(128)S(1)}, f32[128]{0:T(128)S(1)}, u32[]{:S(2)}, u32[]{:S(2)}) collective-permute-start(f32[128]{0:T(128)S(1)} %add_select_fusion.1), channel_id=1, source_target_pairs={{0,8},{1,9},{2,10},{3,11},{4,12},{5,13},{6,14},{7,15},{8,0},{9,1},... | collective-permute-start | bytes 1544 | tf_op jit(solution)/shard_map/ppermute | solution.py:320
  169.6 3.5 %collective-permute-start.10 = (f32[128]{0:T(128)S(1)}, f32[128]{0:T(128)S(1)}, u32[]{:S(2)}, u32[]{:S(2)}) collective-permute-start(f32[128]{0:T(128)S(1)} %add_select_fusion.1), channel_id=1, source_target_pairs={{0,12},{1,13},{2,14},{3,15},{4,0},{5,1},{6,2},{7,3},{8,4},{9,5},{1... | collective-permute-start | bytes 1544 | tf_op jit(solution)/shard_map/ppermute | solution.py:320
  170.7 4.8 %collective-permute-start.8 = (f32[128]{0:T(128)S(1)}, f32[128]{0:T(128)S(1)}, u32[]{:S(2)}, u32[]{:S(2)}) collective-permute-start(f32[128]{0:T(128)S(1)} %add_select_fusion.1), channel_id=1, source_target_pairs={{0,4},{1,5},{2,6},{3,7},{4,8},{5,9},{6,10},{7,11},{8,12},{9,13},{1... | collective-permute-start | bytes 1544 | tf_op jit(solution)/shard_map/ppermute | solution.py:320
  171.8 5.0 %collective-permute-start = (f32[2,64,128]{2,1,0:T(8,128)S(1)}, f32[2,64,128]{2,1,0:T(8,128)S(1)}, u32[]{:S(2)}, u32[]{:S(2)}) collective-permute-start(f32[2,64,128]{2,1,0:T(8,128)S(1)} %get-tuple-element.25), channel_id=1, source_target_pairs={{0,64},{64,0},{1,65},{65,1},{2,66},{66,2},{3,67},{67,3},{4,68},{68... | collective-permute-start | bytes 196616 | tf_op jit(solution)/shard_map/ppermute | solution.py:363
  (3 other events, 3.9 us)

commit v3 on v2

--- a/solution.py
+++ b/solution.py
@@ -10,7 +10,9 @@
 
 STEPS = 28
 LANES = 128
-QT = 256
+QT = 512
+TILE = 256
+CHUNK = 256
 bf16 = jnp.bfloat16
 f32 = jnp.float32
 
@@ -103,7 +105,7 @@
 
 def attend_kernel(which, carried, folded, tok, txt, len_ref, r_ref, *refs):
     c_ref = refs[0] if carried else None
-    o_ref, top_ref, k2, vt, top = refs[-5:]
+    o_ref, top_ref, k2, vt, top, sbuf = refs[-6:]
     shards = r_ref.shape[0]
     hd = LANES // 2
     rows = tok // 2 if folded else tok
@@ -111,7 +113,8 @@
     slot = 16
     n_txt = shards * slot
     t = pl.program_id(0)
-    length = len_ref[which]
+    request = which if which < 2 else (lax.axis_index("seq") % 4) // 2
+    length = len_ref[0, request]
 
     @pl.when(t == 0)
     def _prep():
@@ -167,19 +170,40 @@
     q = r_ref[pl.ds(t * per, per), 0:rows, :].reshape(QT, LANES).astype(f32)
     q = q * (math.log2(math.e) / math.sqrt(hd))
     lane = lax.broadcasted_iota(jnp.int32, (QT, LANES), 1)
-    outs = []
+    queries = []
     for h in range(2):
         qh = jnp.where((lane >= hd) == (h == 1), q, 0.0)
         hi = qh.astype(bf16)
         lo = (qh - hi.astype(f32)).astype(bf16)
-        q2 = jnp.concatenate([hi, lo], axis=1)
-        s = lax.dot_general(k2[...], q2, (((1,), (1,)), ((), ())), preferred_element_type=f32)
-        m = jnp.max(s, axis=0, keepdims=True)
-        p = jnp.exp2(s - m).astype(bf16)
-        o = jnp.dot(vt[h], p, preferred_element_type=f32)
-        outs.append(o[:hd] / o[hd : hd + 1])
-        top[h : h + 1, :] = jnp.maximum(top[h : h + 1, :], m)
-    out = jnp.concatenate(outs, axis=0).T.astype(bf16)
+        queries.append(jnp.concatenate([hi, lo], axis=1))
+    units = [(i, h) for i in range(QT // TILE) for h in range(2)]
+    n_keys = k2.shape[0]
+    outs = {}
+    m = None
+    for u in range(len(units) + 1):
+        if u < len(units):
+            i, h = units[u]
+            qu = queries[h][i * TILE : (i + 1) * TILE]
+        part, acc = None, None
+        for lo in range(0, n_keys, CHUNK):
+            at = slice(lo, lo + CHUNK)
+            if u < len(units):
+                s = lax.dot_general(k2[at, :], qu, (((1,), (1,)), ((), ())), preferred_element_type=f32)
+                sbuf[u % 2, at, :] = s
+                top8 = jnp.max(s.reshape(CHUNK // 8, 8, TILE), axis=0)
+                part = top8 if part is None else jnp.maximum(part, top8)
+            if u > 0:
+                p = jnp.exp2(sbuf[(u - 1) % 2, at, :] - m).astype(bf16)
+                o = jnp.dot(vt[units[u - 1][1], :, at], p, preferred_element_type=f32)
+                acc = o if acc is None else acc + o
+        if u > 0:
+            outs[units[u - 1]] = acc[:hd] / acc[hd : hd + 1]
+        if u < len(units):
+            m = jnp.max(part, axis=0, keepdims=True)
+            top[h : h + 1, :] = jnp.maximum(top[h : h + 1, :], m)
+    out = jnp.concatenate(
+        [jnp.concatenate([outs[i, h] for h in range(2)], axis=0).T.astype(bf16) for i in range(QT // TILE)], axis=0
+    )
     o_ref[:, 0:rows, :] = out.reshape(per, rows, LANES)
     if carried:
         o_ref[:, rows:, :] = c_ref[...]
@@ -217,9 +241,10 @@
         scratch_shapes=[
             pltpu.VMEM((n_keys, 2 * LANES), bf16),
             pltpu.VMEM((2, LANES // 2 + 16, n_keys), bf16),
-            pltpu.VMEM((8, QT), f32),
+            pltpu.VMEM((8, TILE), f32),
+            pltpu.VMEM((2, n_keys, TILE), f32),
         ],
-        compiler_params=pltpu.CompilerParams(vmem_limit_bytes=40 * 1024 * 1024),
+        compiler_params=pltpu.CompilerParams(vmem_limit_bytes=24 * 1024 * 1024),
         cost_estimate=pl.CostEstimate(
             flops=heads * 4 * shards * tok * n_keys * LANES,
             bytes_accessed=4 * shards * total * LANES,
@@ -230,7 +255,7 @@
 
 
 def finish_kernel(
-    n_pairs, half_ref, a_ref, b_ref, hid_ref, gate_ref, mod_ref, ob_ref, fw_ref, w_hbm,
+    n_pairs, guide_ref, a_ref, b_ref, hid_ref, gate_ref, mod_ref, ob_ref, fw_ref, w_hbm,
     pred_ref, sq_ref, att, w, acc, sem,
 ):
     shards, tok, _ = b_ref.shape
@@ -284,10 +309,11 @@
         pred = lax.dot_general(
             fw_ref[...], att[r * tok : (r + 1) * tok, :], (((1,), (1,)), ((), ())), preferred_element_type=f32
         )
-        pred_ref[r] = half_ref[r] * pred
-
-
-def finish(half_weight, ra, rb, hidden_in, gate, mod, out_bias, final_weight, out_weight):
+        cond = lax.axis_index("cfg") == 0
+        pred_ref[r] = jnp.where(cond, guide_ref[r], 1.0 - guide_ref[r]) * pred
+
+
+def finish(guidance, ra, rb, hidden_in, gate, mod, out_bias, final_weight, out_weight):
     shards, tok, _ = rb.shape
     width = out_weight.shape[0]
     c_out = final_weight.shape[0]
@@ -312,7 +338,7 @@
             flops=4 * tok * width * (width + c_out), bytes_accessed=2 * width * width, transcendentals=0
         ),
         name="finish",
-    )(half_weight, ra, rb, hidden_in, gate, mod, out_bias, final_weight, out_weight)
+    )(guidance, ra, rb, hidden_in, gate, mod, out_bias, final_weight, out_weight)
 
 
 def ring_stage(x, axis, size, move, combine):
@@ -339,25 +365,18 @@
     def swap(x):
         return lax.all_to_all(x, "seq", split_axis=0, concat_axis=0, tiled=True)
 
-    length_c = jnp.where((position % 4) // 2 == 0, text_len[0, 0], text_len[0, 1])
-    lengths = jnp.stack([text_len[0, 0], text_len[0, 1], length_c])
-    half_weight = jnp.where(lax.axis_index("cfg") == 0, guidance, 1.0 - guidance)
-    lengths, half_weight, first = lax.optimization_barrier(
-        (lengths, half_weight, pack_single(*streams, shards))
-    )
-
-    in_c = swap(first)
+    in_c = swap(pack_single(*streams, shards))
     in_a = swap(pack_pairs(0, *streams, shards))
-    out_c, top_c = attend(in_c, lengths, 2, tok, txt, True)
+    out_c, top_c = attend(in_c, text_len, 2, tok, txt, True)
     second, out_c = lax.optimization_barrier((pack_pairs(1, *streams, shards), out_c))
     in_b = swap(second)
-    out_a, top_a = attend(in_a, lengths, 0, tok, txt, False, out_c)
+    out_a, top_a = attend(in_a, text_len, 0, tok, txt, False, out_c)
     back_a = swap(out_a)
-    out_b, top_b = attend(in_b, lengths, 1, tok, txt, False)
+    out_b, top_b = attend(in_b, text_len, 1, tok, txt, False)
     back_b = swap(out_b)
 
     pred, squares = finish(
-        half_weight, back_a, back_b, hidden_in, attn_gate, final_mod,
+        guidance, back_a, back_b, hidden_in, attn_gate, final_mod,
         out_bias[None], final_weight.T, out_weight,
     )
     velocity = pred + lax.ppermute(pred, "cfg", [(0, 1), (1, 0)]) + final_bias[None, :, None]

time: 179 us -> 157 us (0.88)
  Pallas kernels: 85.7 us -> 63.8 us
  waiting for transfers between devices: 33.2 us -> 40.8 us
  starting transfers between devices: 41.8 us -> 38.3 us
  other arithmetic: 6.94 us -> 4.91 us
    pallas_call x3, Pallas kernels: 63.5 us -> 41.6 us  [attend(): pl.pallas_call(functools.partial(attend_kernel, which, carry is not None,...]
    all_to_all x5, waiting for transfers between devices: 21.1 us -> 28.7 us  [swap(): return lax.all_to_all(x, 'seq', split_axis=0, concat_axis=0, tiled=True)]
    all_to_all x5, starting transfers between devices: 29.7 us -> 26.1 us  [swap(): return lax.all_to_all(x, 'seq', split_axis=0, concat_axis=0, tiled=True)]
    unnamed x22 -> x30, local copies, waits for them, and re-layouts: 3.96 us -> 4.72 us
  transfers between devices with their start and end apart: 16 -> 16, of which waited for: 10 -> 11; matrix products, arithmetic and copies ran while one was open for 3% -> 3% of each run, Pallas kernels for 40% -> 32%
where the time goes in v3:
time: 157 us; the launch traced here: 156 us
  Pallas kernels  63.8 us (41%)
  waiting for transfers between devices  40.8 us (26%)
  starting transfers between devices  38.3 us (24%)
  local copies, waits for them, and re-layouts  5.88 us (4%)
  other arithmetic  4.91 us (3%)
  between operations  2.19 us (1%)
    pallas_call x3, Pallas kernels, attend(): pl.pallas_call(functools.partial(attend_kernel, which, carry is not None,...  41.6 us
    all_to_all x5, waiting for transfers between devices, swap(): return lax.all_to_all(x, 'seq', split_axis=0, concat_axis=0, tiled=True)  28.7 us
    all_to_all x5, starting transfers between devices, swap(): return lax.all_to_all(x, 'seq', split_axis=0, concat_axis=0, tiled=True)  26.1 us
    ppermute x9, waiting for transfers between devices, ring_stage(): others = [lax.ppermute(x, axis, p) for p in pairs]  12.1 us
    ppermute x9, starting transfers between devices, ring_stage(): others = [lax.ppermute(x, axis, p) for p in pairs]  12 us
    pallas_call x1, Pallas kernels, finish(): pl.pallas_call(functools.partial(finish_kernel, n_pairs), in_specs=[pl.Bl...  11.5 us
    pallas_call x2, Pallas kernels, pack_pairs(): pl.pallas_call(functools.partial(pack_pairs_kernel, r), grid=(shards // p...  7.67 us
    unnamed x30, local copies, waits for them, and re-layouts  4.72 us
  transfers between devices with their start and end apart: 16, of which 11 were waited for; matrix products, arithmetic and copies ran while one was open for 3% of the time, Pallas kernels for 32%

profile of v3, /device:TPU:0, one launch (start us, length us, event | category | flops | bytes accessed | tf_op | source)
XLA Modules:
  0.0 155.8 jit_solution(8024471232612060285)
XLA Ops:
  0.6 3.1 %pack_single.1 = bf16[16,212,128]{2,1,0:T(8,128)(2,1)} custom-call(bf16[1,2,128,2432]{3,2,1,0:T(8,128)(2,1)} %q_ref.5, bf16[1,2,128,2432]{3,2,1,0:T(8,128)(2,1)} %k_ref.5, bf16[1,2,128,2432]{3,2,1,0:T(8,128)(2,1)} %v_ref.5, bf16[1,10,2,2432]{3,2,1,0:T(2,128)(2,1)} %bitcast.19, bf16[1,10,2,2432]{3,2,1,0:T(2,128)(2,1)} %bitcast.22), custom_call_target="tpu_custom_call" | custom-call | bytes 1736704 | tf_op jit(solution)/shard_map/pack_single/pallas_call | solution.py:95
  3.7 8.0 %all-to-all-start.1 = ((bf16[16,212,128]{2,1,0:T(8,128)(2,1)}), bf16[16,212,128]{2,1,0:T(8,128)(2,1)S(1)}, u32[]{:S(2)}, u32[]{:S(2)}) async-start(bf16[16,212,128]{2,1,0:T(8,128)(2,1)} %pack_single.1), calls=%async_computation.1 | async-start | bytes 1769472 | tf_op jit(solution)/shard_map/all_to_all | solution.py:366
  11.7 3.8 %pack_pairs.2 = bf16[16,404,128]{2,1,0:T(8,128)(2,1)} custom-call(bf16[1,2,128,2432]{3,2,1,0:T(8,128)(2,1)} %q_ref.5, bf16[1,2,128,2432]{3,2,1,0:T(8,128)(2,1)} %k_ref.5, bf16[1,2,128,2432]{3,2,1,0:T(8,128)(2,1)} %v_ref.5, bf16[1,10,2,2432]{3,2,1,0:T(2,128)(2,1)} %bitcast.20, bf16[1,10,2,2432]{3,2,1,0:T(2,128)(2,1)} %bitcast.23), custom_call_target="tpu_custom_call" | custom-call | bytes 3309568 | tf_op jit(solution)/shard_map/pack_pairs/pallas_call | solution.py:47
  15.5 11.8 %all-to-all-done.1.r_ref = bf16[16,212,128]{2,1,0:T(8,128)(2,1)S(1)} async-done(((bf16[16,212,128]{2,1,0:T(8,128)(2,1)}), bf16[16,212,128]{2,1,0:T(8,128)(2,1)S(1)}, u32[]{:S(2)}, u32[]{:S(2)}) %all-to-all-start.1) | async-done | bytes 868384 | tf_op jit(solution)/shard_map/all_to_all | solution.py:366
  27.3 3.7 %all-to-all-start = ((bf16[16,404,128]{2,1,0:T(8,128)(2,1)}), bf16[16,404,128]{2,1,0:T(8,128)(2,1)S(1)}, u32[]{:S(2)}, u32[]{:S(2)}) async-start(bf16[16,404,128]{2,1,0:T(8,128)(2,1)} %pack_pairs.2), calls=%async_computation | async-start | bytes 3342336 | tf_op jit(solution)/shard_map/all_to_all | solution.py:366
  31.1 3.8 %pack_pairs.3 = bf16[16,404,128]{2,1,0:T(8,128)(2,1)} custom-call(bf16[1,2,128,2432]{3,2,1,0:T(8,128)(2,1)} %q_ref.5, bf16[1,2,128,2432]{3,2,1,0:T(8,128)(2,1)} %k_ref.5, bf16[1,2,128,2432]{3,2,1,0:T(8,128)(2,1)} %v_ref.5, bf16[1,10,2,2432]{3,2,1,0:T(2,128)(2,1)} %bitcast.21, bf16[1,10,2,2432]{3,2,1,0:T(2,128)(2,1)} %bitcast.24), custom_call_target="tpu_custom_call" | custom-call | bytes 3309568 | tf_op jit(solution)/shard_map/pack_pairs/pallas_call | solution.py:47
  34.9 8.6 %attend_single.1 = (bf16[16,64,128]{2,1,0:T(8,128)(2,1)S(1)}, f32[8,128]{1,0:T(8,128)S(1)}) custom-call(s32[1,2]{1,0:T(1,128)S(1)} %copy-done.7, bf16[16,212,128]{2,1,0:T(8,128)(2,1)S(1)} %all-to-all-done.1.r_ref), custom_call_target="tpu_custom_call" | custom-call | flops 2415919104 | bytes 1736704 | tf_op jit(solution)/shard_map/attend_single/pallas_call | solution.py:225
  44.3 10.2 %all-to-all-done.r_ref = bf16[16,404,128]{2,1,0:T(8,128)(2,1)S(1)} async-done(((bf16[16,404,128]{2,1,0:T(8,128)(2,1)}), bf16[16,404,128]{2,1,0:T(8,128)(2,1)S(1)}, u32[]{:S(2)}, u32[]{:S(2)}) %all-to-all-start) | async-done | bytes 1654816 | tf_op jit(solution)/shard_map/all_to_all | solution.py:366
  54.5 3.7 %all-to-all-start.3 = ((bf16[16,404,128]{2,1,0:T(8,128)(2,1)}), bf16[16,404,128]{2,1,0:T(8,128)(2,1)S(1)}, u32[]{:S(2)}, u32[]{:S(2)}) async-start(bf16[16,404,128]{2,1,0:T(8,128)(2,1)} %pack_pairs.3), calls=%async_computation.3 | async-start | bytes 3342336 | tf_op jit(solution)/shard_map/all_to_all | solution.py:366
  61.0 16.5 %attend_pair.2 = (bf16[16,192,128]{2,1,0:T(8,128)(2,1)S(1)}, f32[8,128]{1,0:T(8,128)S(1)}) custom-call(s32[1,2]{1,0:T(1,128)S(1)} %copy-done.7, bf16[16,404,128]{2,1,0:T(8,128)(2,1)S(1)} %all-to-all-done.r_ref, bf16[16,64,128]{2,1,0:T(8,128)(2,1)S(1)} %copy-done.9), custom_call_target="tpu_custom_call" | custom-call | flops 4831838208 | bytes 3309568 | tf_op jit(solution)/shard_map/attend_pair/pallas_call | solution.py:225
  78.4 4.2 %all-to-all-done.3.r_ref = bf16[16,404,128]{2,1,0:T(8,128)(2,1)S(1)} async-done(((bf16[16,404,128]{2,1,0:T(8,128)(2,1)}), bf16[16,404,128]{2,1,0:T(8,128)(2,1)S(1)}, u32[]{:S(2)}, u32[]{:S(2)}) %all-to-all-start.3) | async-done | bytes 1654816 | tf_op jit(solution)/shard_map/all_to_all | solution.py:366
  82.6 3.8 %all-to-all-start.2 = ((bf16[16,192,128]{2,1,0:T(8,128)(2,1)}), bf16[16,192,128]{2,1,0:T(8,128)(2,1)S(1)}, u32[]{:S(2)}, u32[]{:S(2)}) async-start(bf16[16,192,128]{2,1,0:T(8,128)(2,1)} %copy-done.1), calls=%async_computation.2 | async-start | bytes 1572864 | tf_op jit(solution)/shard_map/all_to_all | solution.py:366
  86.5 16.5 %attend_pair.3 = (bf16[16,128,128]{2,1,0:T(8,128)(2,1)S(1)}, f32[8,128]{1,0:T(8,128)S(1)}) custom-call(s32[1,2]{1,0:T(1,128)S(1)} %copy-done.7, bf16[16,404,128]{2,1,0:T(8,128)(2,1)S(1)} %all-to-all-done.3.r_ref), custom_call_target="tpu_custom_call" | custom-call | flops 4831838208 | bytes 3309568 | tf_op jit(solution)/shard_map/attend_pair/pallas_call | solution.py:225
  105.7 7.0 %all-to-all-start.4 = ((bf16[16,128,128]{2,1,0:T(8,128)(2,1)}), bf16[16,128,128]{2,1,0:T(8,128)(2,1)S(1)}, u32[]{:S(2)}, u32[]{:S(2)}) async-start(bf16[16,128,128]{2,1,0:T(8,128)(2,1)} %copy-done.2), calls=%async_computation.4 | async-start | bytes 1048576 | tf_op jit(solution)/shard_map/all_to_all | solution.py:366
  112.7 1.3 fusion.5
  114.0 3.1 %collective-permute-start.4 = (f32[128]{0:T(128)S(1)}, f32[128]{0:T(128)S(1)}, u32[]{:S(2)}, u32[]{:S(2)}) collective-permute-start(f32[128]{0:T(128)S(1)} %fusion.5), channel_id=1, source_target_pairs={{0,48},{16,0},{32,16},{48,32},{1,49},{17,1},{33,17},{49,33},{2,50}... | collective-permute-start | bytes 1544 | tf_op jit(solution)/shard_map/ppermute | solution.py:346
  118.8 3.4 %collective-permute-done.3 = f32[128]{0:T(128)S(1)} collective-permute-done((f32[128]{0:T(128)S(1)}, f32[128]{0:T(128)S(1)}, u32[]{:S(2)}, u32[]{:S(2)}) %collective-permute-start.3) | collective-permute-done | bytes 544 | tf_op jit(solution)/shard_map/ppermute | solution.py:346
  122.5 2.4 %all-to-all-done.4.b_ref = bf16[16,128,128]{2,1,0:T(8,128)(2,1)S(1)} async-done(((bf16[16,128,128]{2,1,0:T(8,128)(2,1)}), bf16[16,128,128]{2,1,0:T(8,128)(2,1)S(1)}, u32[]{:S(2)}, u32[]{:S(2)}) %all-to-all-start.4) | async-done | bytes 524320 | tf_op jit(solution)/shard_map/all_to_all | solution.py:366
  126.2 11.5 %finish.1 = (f32[2,64,128]{2,1,0:T(8,128)S(1)}, f32[8,128]{1,0:T(8,128)S(1)}) custom-call(f32[2]{0:T(128)S(1)} %copy-done.6, bf16[16,192,128]{2,1,0:T(8,128)(2,1)S(1)} %all-to-all-done.2.a_ref, bf16[16,128,128]{2,1,0:T(8,128)(2,1)S(1)} %all-to-all-done.4.b_ref, bf16[1,2,128,2432]{3,2,1,0:T(8,128)(2,1)S(1)} %copy-done, f32[1,2,2432]{2,1,0:T(2,128)S(1)} %copy-done.5, ...), custom_call_target="tpu_custom_call" | custom-call | flops 3107979264 | bytes 11829248 | tf_op jit(solution)/shard_map/finish/pallas_call | solution.py:322
  139.0 2.2 %collective-permute-start.7 = (f32[128]{0:T(128)S(1)}, f32[128]{0:T(128)S(1)}, u32[]{:S(2)}, u32[]{:S(2)}) collective-permute-start(f32[128]{0:T(128)S(1)} %pad_maximum_fusion), channel_id=1, source_target_pairs={{0,3},{1,0},{2,1},{3,2},{4,7},{5,4},{6,5},{7,6},{8,11},{9,8},{10,9... | collective-permute-start | bytes 1544 | tf_op jit(solution)/shard_map/ppermute | solution.py:346
  141.1 1.8 %collective-permute-done.6 = f32[128]{0:T(128)S(1)} collective-permute-done((f32[128]{0:T(128)S(1)}, f32[128]{0:T(128)S(1)}, u32[]{:S(2)}, u32[]{:S(2)}) %collective-permute-start.6) | collective-permute-done | bytes 544 | tf_op jit(solution)/shard_map/ppermute | solution.py:346
  142.9 2.9 %collective-permute-done.5 = f32[128]{0:T(128)S(1)} collective-permute-done((f32[128]{0:T(128)S(1)}, f32[128]{0:T(128)S(1)}, u32[]{:S(2)}, u32[]{:S(2)}) %collective-permute-start.5) | collective-permute-done | bytes 544 | tf_op jit(solution)/shard_map/ppermute | solution.py:346
  145.9 2.0 %collective-permute-start.9 = (f32[128]{0:T(128)S(1)}, f32[128]{0:T(128)S(1)}, u32[]{:S(2)}, u32[]{:S(2)}) collective-permute-start(f32[128]{0:T(128)S(1)} %add_select_fusion.1), channel_id=1, source_target_pairs={{0,8},{1,9},{2,10},{3,11},{4,12},{5,13},{6,14},{7,15},{8,0},{9,1},... | collective-permute-start | bytes 1544 | tf_op jit(solution)/shard_map/ppermute | solution.py:346
  151.4 2.4 %collective-permute-done.8 = f32[128]{0:T(128)S(1)} collective-permute-done((f32[128]{0:T(128)S(1)}, f32[128]{0:T(128)S(1)}, u32[]{:S(2)}, u32[]{:S(2)}) %collective-permute-start.8) | collective-permute-done | bytes 544 | tf_op jit(solution)/shard_map/ppermute | solution.py:346
  (63 shorter events, 16.0 us)
Async XLA Ops:
  3.7 23.6 %all-to-all-start.1 = ((bf16[16,212,128]{2,1,0:T(8,128)(2,1)}), bf16[16,212,128]{2,1,0:T(8,128)(2,1)S(1)}, u32[]{:S(2)}, u32[]{:S(2)}) async-start(bf16[16,212,128]{2,1,0:T(8,128)(2,1)} %pack_single.1), calls=%async_computation.1 | async-start | bytes 1769472 | tf_op jit(solution)/shard_map/all_to_all | solution.py:366
  27.3 27.2 %all-to-all-start = ((bf16[16,404,128]{2,1,0:T(8,128)(2,1)}), bf16[16,404,128]{2,1,0:T(8,128)(2,1)S(1)}, u32[]{:S(2)}, u32[]{:S(2)}) async-start(bf16[16,404,128]{2,1,0:T(8,128)(2,1)} %pack_pairs.2), calls=%async_computation | async-start | bytes 3342336 | tf_op jit(solution)/shard_map/all_to_all | solution.py:366
  54.5 28.1 %all-to-all-start.3 = ((bf16[16,404,128]{2,1,0:T(8,128)(2,1)}), bf16[16,404,128]{2,1,0:T(8,128)(2,1)S(1)}, u32[]{:S(2)}, u32[]{:S(2)}) async-start(bf16[16,404,128]{2,1,0:T(8,128)(2,1)} %pack_pairs.3), calls=%async_computation.3 | async-start | bytes 3342336 | tf_op jit(solution)/shard_map/all_to_all | solution.py:366
  82.6 23.1 %all-to-all-start.2 = ((bf16[16,192,128]{2,1,0:T(8,128)(2,1)}), bf16[16,192,128]{2,1,0:T(8,128)(2,1)S(1)}, u32[]{:S(2)}, u32[]{:S(2)}) async-start(bf16[16,192,128]{2,1,0:T(8,128)(2,1)} %copy-done.1), calls=%async_computation.2 | async-start | bytes 1572864 | tf_op jit(solution)/shard_map/all_to_all | solution.py:366
  86.4 32.3 %copy-start.14 = (s32[2]{0:T(128)S(1)}, s32[2]{0:T(128)}, u32[]{:S(2)}) copy-start(s32[2]{0:T(128)} %param.32) | copy-start | bytes 28
  86.4 32.3 %copy-start.11 = (f32[2432]{0:T(1024)S(1)}, f32[2432]{0:T(1024)}, u32[]{:S(2)}) copy-start(f32[2432]{0:T(1024)} %param.27) | copy-start | bytes 29188
  86.4 38.4 %copy-start.3 = (bf16[2432,64]{0,1:T(8,128)(2,1)S(1)}, bf16[2432,64]{0,1:T(8,128)(2,1)}, u32[]{:S(2)}) copy-start(bf16[2432,64]{0,1:T(8,128)(2,1)} %param.30) | copy-start | bytes 933892
  86.5 38.4 %copy-start.4 = (f32[1,2,2,2432]{3,2,1,0:T(2,128)S(1)}, f32[1,2,2,2432]{3,2,1,0:T(2,128)}, u32[]{:S(2)}) copy-start(f32[1,2,2,2432]{3,2,1,0:T(2,128)} %mod_ref.1) | copy-start | bytes 116740
  86.5 38.4 %copy-start.5 = (f32[1,2,2432]{2,1,0:T(2,128)S(1)}, f32[1,2,2432]{2,1,0:T(2,128)}, u32[]{:S(2)}) copy-start(f32[1,2,2432]{2,1,0:T(2,128)} %gate_ref.1) | copy-start | bytes 58372
  86.5 38.4 %copy-start.6 = (f32[2]{0:T(128)S(1)}, f32[2]{0:T(128)}, u32[]{:S(2)}) copy-start(f32[2]{0:T(128)} %guide_ref.1) | copy-start | bytes 28
  105.6 7.1 %collective-permute-start.1 = (f32[128]{0:T(128)S(1)}, f32[128]{0:T(128)S(1)}, u32[]{:S(2)}, u32[]{:S(2)}) collective-permute-start(f32[128]{0:T(128)S(1)} %and_select_fusion), channel_id=1, source_target_pairs={{0,64},{64,0},{1,65},{65,1},{2,66},{66,2},{3,67},{67,3},{4,68},{68... | collective-permute-start | bytes 1544 | tf_op jit(solution)/shard_map/ppermute | solution.py:395
  105.7 19.2 %all-to-all-start.4 = ((bf16[16,128,128]{2,1,0:T(8,128)(2,1)}), bf16[16,128,128]{2,1,0:T(8,128)(2,1)S(1)}, u32[]{:S(2)}, u32[]{:S(2)}) async-start(bf16[16,128,128]{2,1,0:T(8,128)(2,1)} %copy-done.2), calls=%async_computation.4 | async-start | bytes 1048576 | tf_op jit(solution)/shard_map/all_to_all | solution.py:366
  114.0 4.8 %collective-permute-start.4 = (f32[128]{0:T(128)S(1)}, f32[128]{0:T(128)S(1)}, u32[]{:S(2)}, u32[]{:S(2)}) collective-permute-start(f32[128]{0:T(128)S(1)} %fusion.5), channel_id=1, source_target_pairs={{0,48},{16,0},{32,16},{48,32},{1,49},{17,1},{33,17},{49,33},{2,50}... | collective-permute-start | bytes 1544 | tf_op jit(solution)/shard_map/ppermute | solution.py:346
  117.1 5.0 %collective-permute-start.3 = (f32[128]{0:T(128)S(1)}, f32[128]{0:T(128)S(1)}, u32[]{:S(2)}, u32[]{:S(2)}) collective-permute-start(f32[128]{0:T(128)S(1)} %fusion.5), channel_id=1, source_target_pairs={{0,32},{16,48},{32,0},{48,16},{1,33},{17,49},{33,1},{49,17},{2,34}... | collective-permute-start | bytes 1544 | tf_op jit(solution)/shard_map/ppermute | solution.py:346
  117.7 4.8 %collective-permute-start.2 = (f32[128]{0:T(128)S(1)}, f32[128]{0:T(128)S(1)}, u32[]{:S(2)}, u32[]{:S(2)}) collective-permute-start(f32[128]{0:T(128)S(1)} %fusion.5), channel_id=1, source_target_pairs={{0,16},{16,32},{32,48},{48,0},{1,17},{17,33},{33,49},{49,1},{2,18}... | collective-permute-start | bytes 1544 | tf_op jit(solution)/shard_map/ppermute | solution.py:346
  126.2 28.9 %copy-start.10 = (f32[2,128,64]{1,2,0:T(8,128)S(1)}, f32[2,128,64]{1,2,0:T(8,128)}, u32[]{:S(2)}) copy-start(f32[2,128,64]{1,2,0:T(8,128)} %param.17) | copy-start | bytes 196612
  126.2 28.9 %copy-start.12 = (f32[64]{0:T(128)S(1)}, f32[64]{0:T(128)}, u32[]{:S(2)}) copy-start(f32[64]{0:T(128)} %param.31) | copy-start | bytes 772
  137.9 5.1 %collective-permute-start.6 = (f32[128]{0:T(128)S(1)}, f32[128]{0:T(128)S(1)}, u32[]{:S(2)}, u32[]{:S(2)}) collective-permute-start(f32[128]{0:T(128)S(1)} %pad_maximum_fusion), channel_id=1, source_target_pairs={{0,2},{1,3},{2,0},{3,1},{4,6},{5,7},{6,4},{7,5},{8,10},{9,11},{10,... | collective-permute-start | bytes 1544 | tf_op jit(solution)/shard_map/ppermute | solution.py:346
  139.0 4.0 %collective-permute-start.7 = (f32[128]{0:T(128)S(1)}, f32[128]{0:T(128)S(1)}, u32[]{:S(2)}, u32[]{:S(2)}) collective-permute-start(f32[128]{0:T(128)S(1)} %pad_maximum_fusion), channel_id=1, source_target_pairs={{0,3},{1,0},{2,1},{3,2},{4,7},{5,4},{6,5},{7,6},{8,11},{9,8},{10,9... | collective-permute-start | bytes 1544 | tf_op jit(solution)/shard_map/ppermute | solution.py:346
  141.1 4.8 %collective-permute-start.5 = (f32[128]{0:T(128)S(1)}, f32[128]{0:T(128)S(1)}, u32[]{:S(2)}, u32[]{:S(2)}) collective-permute-start(f32[128]{0:T(128)S(1)} %pad_maximum_fusion), channel_id=1, source_target_pairs={{0,1},{1,2},{2,3},{3,0},{4,5},{5,6},{6,7},{7,4},{8,9},{9,10},{10,1... | collective-permute-start | bytes 1544 | tf_op jit(solution)/shard_map/ppermute | solution.py:346
  145.9 5.0 %collective-permute-start.9 = (f32[128]{0:T(128)S(1)}, f32[128]{0:T(128)S(1)}, u32[]{:S(2)}, u32[]{:S(2)}) collective-permute-start(f32[128]{0:T(128)S(1)} %add_select_fusion.1), channel_id=1, source_target_pairs={{0,8},{1,9},{2,10},{3,11},{4,12},{5,13},{6,14},{7,15},{8,0},{9,1},... | collective-permute-start | bytes 1544 | tf_op jit(solution)/shard_map/ppermute | solution.py:346
  147.9 3.5 %collective-permute-start.10 = (f32[128]{0:T(128)S(1)}, f32[128]{0:T(128)S(1)}, u32[]{:S(2)}, u32[]{:S(2)}) collective-permute-start(f32[128]{0:T(128)S(1)} %add_select_fusion.1), channel_id=1, source_target_pairs={{0,12},{1,13},{2,14},{3,15},{4,0},{5,1},{6,2},{7,3},{8,4},{9,5},{1... | collective-permute-start | bytes 1544 | tf_op jit(solution)/shard_map/ppermute | solution.py:346
  149.0 4.8 %collective-permute-start.8 = (f32[128]{0:T(128)S(1)}, f32[128]{0:T(128)S(1)}, u32[]{:S(2)}, u32[]{:S(2)}) collective-permute-start(f32[128]{0:T(128)S(1)} %add_select_fusion.1), channel_id=1, source_target_pairs={{0,4},{1,5},{2,6},{3,7},{4,8},{5,9},{6,10},{7,11},{8,12},{9,13},{1... | collective-permute-start | bytes 1544 | tf_op jit(solution)/shard_map/ppermute | solution.py:346
  150.1 5.0 %collective-permute-start = (f32[2,64,128]{2,1,0:T(8,128)S(1)}, f32[2,64,128]{2,1,0:T(8,128)S(1)}, u32[]{:S(2)}, u32[]{:S(2)}) collective-permute-start(f32[2,64,128]{2,1,0:T(8,128)S(1)} %get-tuple-element.19), channel_id=1, source_target_pairs={{0,64},{64,0},{1,65},{65,1},{2,66},{66,2},{3,67},{67,3},{4,68},{68... | collective-permute-start | bytes 196616 | tf_op jit(solution)/shard_map/ppermute | solution.py:382
  (7 other events, 32.3 us)

commit v4 on v3

--- a/solution.py
+++ b/solution.py
@@ -341,10 +341,12 @@
     )(guidance, ra, rb, hidden_in, gate, mod, out_bias, final_weight, out_weight)
 
 
-def ring_stage(x, axis, size, move, combine):
-    pairs = [[(i, move(i, k)) for i in range(size)] for k in (1, 2, 3)]
-    others = [lax.ppermute(x, axis, p) for p in pairs]
-    return combine(combine(x, others[0]), combine(others[1], others[2]))
+def exchange(x, axis, size, combine):
+    step = 1
+    while step < size:
+        x = combine(x, lax.ppermute(x, axis, [(i, i ^ step) for i in range(size)]))
+        step *= 2
+    return x
 
 
 def local(
@@ -385,23 +387,22 @@
     velocity, latent_next = velocity.transpose(0, 2, 1), latent_next.transpose(0, 2, 1)
 
     lane = jnp.arange(LANES, dtype=jnp.int32)
-    pair_top = jnp.maximum(top_a[0:2, 0], top_b[0:2, 0])
-    single_top = jnp.maximum(top_c[0, 0], top_c[1, 0])
+    pair_top = jnp.maximum(top_a[0:2], top_b[0:2])
+    single_top = jnp.maximum(top_c[0], top_c[1])
     single_head = 2 * shards + 2 * (position // 4) + position % 2
     table = jnp.full((LANES,), -jnp.inf, f32)
     table = jnp.where(lane == 2 * position, pair_top[0], table)
     table = jnp.where(lane == 2 * position + 1, pair_top[1], table)
     table = jnp.where((lane == single_head) & (single_head < head_count), single_top, table)
-    table = jnp.maximum(table, lax.ppermute(table, "cfg", [(0, 1), (1, 0)]))
-    table = ring_stage(table, "req", 4, lambda i, k: (i + k) % 4, jnp.maximum)
-
-    small = jnp.concatenate([table[: LANES - 2], squares[0:2, 0]])
+    table = exchange(table, "cfg", 2, jnp.maximum)
+    table = exchange(table, "req", 4, jnp.maximum)
+
+    small = jnp.where(lane == LANES - 2, squares[0], jnp.where(lane == LANES - 1, squares[1], table))
 
     def combine(a, b):
         return jnp.where(lane < LANES - 2, jnp.maximum(a, b), a + b)
 
-    small = ring_stage(small, "seq", shards, lambda i, k: i // 4 * 4 + (i + k) % 4, combine)
-    small = ring_stage(small, "seq", shards, lambda i, k: (i + 4 * k) % shards, combine)
+    small = exchange(small, "seq", shards, combine)
     hidden_norms = jnp.sqrt(small[LANES - 2 :] / (image_rows * model_width))[None, :]
 
     own_slots = position * per_shard + jnp.arange(per_shard, dtype=jnp.int32)

time: 157 us -> 155 us (0.987)
  waiting for transfers between devices: 40.8 us -> 48.6 us
  starting transfers between devices: 38.3 us -> 33.4 us
  other arithmetic: 4.91 us -> 2.26 us
    ppermute x10 -> x7, waiting for transfers between devices: 12.1 us -> 17.7 us  [exchange(): x = combine(x, lax.ppermute(x, axis, [(i, i ^ step) for i in range(size)]))]
    ppermute x10 -> x7, starting transfers between devices: 12.1 us -> 7.13 us  [exchange(): x = combine(x, lax.ppermute(x, axis, [(i, i ^ step) for i in range(size)]))]
    all_to_all x5, waiting for transfers between devices: 28.7 us -> 30.9 us  [swap(): return lax.all_to_all(x, 'seq', split_axis=0, concat_axis=0, tiled=True)]
  transfers between devices with their start and end apart: 16 -> 13, of which waited for: 11 -> 10; matrix products, arithmetic and copies ran while one was open for 3% -> 1% of each run, Pallas kernels for 32% -> 40%
where the time goes in v4:
time: 155 us; the launch traced here: 154 us
  Pallas kernels  63.8 us (41%)
  waiting for transfers between devices  48.6 us (31%)
  starting transfers between devices  33.4 us (22%)
  local copies, waits for them, and re-layouts  4.73 us (3%)
  other arithmetic  2.26 us (1%)
    pallas_call x3, Pallas kernels, attend(): pl.pallas_call(functools.partial(attend_kernel, which, carry is not None,...  41.5 us
    all_to_all x5, waiting for transfers between devices, swap(): return lax.all_to_all(x, 'seq', split_axis=0, concat_axis=0, tiled=True)  30.9 us
    all_to_all x5, starting transfers between devices, swap(): return lax.all_to_all(x, 'seq', split_axis=0, concat_axis=0, tiled=True)  26.1 us
    ppermute x7, waiting for transfers between devices, exchange(): x = combine(x, lax.ppermute(x, axis, [(i, i ^ step) for i in range(size)]))  17.7 us
    pallas_call x1, Pallas kernels, finish(): pl.pallas_call(functools.partial(finish_kernel, n_pairs), in_specs=[pl.Bl...  11.5 us
    pallas_call x2, Pallas kernels, pack_pairs(): pl.pallas_call(functools.partial(pack_pairs_kernel, r), grid=(shards // p...  7.7 us
    ppermute x7, starting transfers between devices, exchange(): x = combine(x, lax.ppermute(x, axis, [(i, i ^ step) for i in range(size)]))  7.13 us
    unnamed x30, local copies, waits for them, and re-layouts  4.72 us
  transfers between devices with their start and end apart: 13, of which 10 were waited for; matrix products, arithmetic and copies ran while one was open for 1% of the time, Pallas kernels for 40%

profile of v4, /device:TPU:0, one launch (start us, length us, event | category | flops | bytes accessed | tf_op | source)
XLA Modules:
  0.0 153.7 jit_solution(17659739235182908935)
XLA Ops:
  0.6 3.1 %pack_single.1 = bf16[16,212,128]{2,1,0:T(8,128)(2,1)} custom-call(bf16[1,2,128,2432]{3,2,1,0:T(8,128)(2,1)} %q_ref.5, bf16[1,2,128,2432]{3,2,1,0:T(8,128)(2,1)} %k_ref.5, bf16[1,2,128,2432]{3,2,1,0:T(8,128)(2,1)} %v_ref.5, bf16[1,10,2,2432]{3,2,1,0:T(2,128)(2,1)} %bitcast.25, bf16[1,10,2,2432]{3,2,1,0:T(2,128)(2,1)} %bitcast.28), custom_call_target="tpu_custom_call" | custom-call | bytes 1736704 | tf_op jit(solution)/shard_map/pack_single/pallas_call | solution.py:95
  3.7 8.0 %all-to-all-start.1 = ((bf16[16,212,128]{2,1,0:T(8,128)(2,1)}), bf16[16,212,128]{2,1,0:T(8,128)(2,1)S(1)}, u32[]{:S(2)}, u32[]{:S(2)}) async-start(bf16[16,212,128]{2,1,0:T(8,128)(2,1)} %pack_single.1), calls=%async_computation.1 | async-start | bytes 1769472 | tf_op jit(solution)/shard_map/all_to_all | solution.py:368
  11.7 3.9 %pack_pairs.2 = bf16[16,404,128]{2,1,0:T(8,128)(2,1)} custom-call(bf16[1,2,128,2432]{3,2,1,0:T(8,128)(2,1)} %q_ref.5, bf16[1,2,128,2432]{3,2,1,0:T(8,128)(2,1)} %k_ref.5, bf16[1,2,128,2432]{3,2,1,0:T(8,128)(2,1)} %v_ref.5, bf16[1,10,2,2432]{3,2,1,0:T(2,128)(2,1)} %bitcast.26, bf16[1,10,2,2432]{3,2,1,0:T(2,128)(2,1)} %bitcast.29), custom_call_target="tpu_custom_call" | custom-call | bytes 3309568 | tf_op jit(solution)/shard_map/pack_pairs/pallas_call | solution.py:47
  15.5 11.8 %all-to-all-done.1.r_ref = bf16[16,212,128]{2,1,0:T(8,128)(2,1)S(1)} async-done(((bf16[16,212,128]{2,1,0:T(8,128)(2,1)}), bf16[16,212,128]{2,1,0:T(8,128)(2,1)S(1)}, u32[]{:S(2)}, u32[]{:S(2)}) %all-to-all-start.1) | async-done | bytes 868384 | tf_op jit(solution)/shard_map/all_to_all | solution.py:368
  27.3 3.7 %all-to-all-start = ((bf16[16,404,128]{2,1,0:T(8,128)(2,1)}), bf16[16,404,128]{2,1,0:T(8,128)(2,1)S(1)}, u32[]{:S(2)}, u32[]{:S(2)}) async-start(bf16[16,404,128]{2,1,0:T(8,128)(2,1)} %pack_pairs.2), calls=%async_computation | async-start | bytes 3342336 | tf_op jit(solution)/shard_map/all_to_all | solution.py:368
  31.1 3.8 %pack_pairs.3 = bf16[16,404,128]{2,1,0:T(8,128)(2,1)} custom-call(bf16[1,2,128,2432]{3,2,1,0:T(8,128)(2,1)} %q_ref.5, bf16[1,2,128,2432]{3,2,1,0:T(8,128)(2,1)} %k_ref.5, bf16[1,2,128,2432]{3,2,1,0:T(8,128)(2,1)} %v_ref.5, bf16[1,10,2,2432]{3,2,1,0:T(2,128)(2,1)} %bitcast.27, bf16[1,10,2,2432]{3,2,1,0:T(2,128)(2,1)} %bitcast.30), custom_call_target="tpu_custom_call" | custom-call | bytes 3309568 | tf_op jit(solution)/shard_map/pack_pairs/pallas_call | solution.py:47
  34.9 8.6 %attend_single.1 = (bf16[16,64,128]{2,1,0:T(8,128)(2,1)S(1)}, f32[8,128]{1,0:T(8,128)S(1)}) custom-call(s32[1,2]{1,0:T(1,128)S(1)} %copy-done.7, bf16[16,212,128]{2,1,0:T(8,128)(2,1)S(1)} %all-to-all-done.1.r_ref), custom_call_target="tpu_custom_call" | custom-call | flops 2415919104 | bytes 1736704 | tf_op jit(solution)/shard_map/attend_single/pallas_call | solution.py:225
  44.3 10.2 %all-to-all-done.r_ref = bf16[16,404,128]{2,1,0:T(8,128)(2,1)S(1)} async-done(((bf16[16,404,128]{2,1,0:T(8,128)(2,1)}), bf16[16,404,128]{2,1,0:T(8,128)(2,1)S(1)}, u32[]{:S(2)}, u32[]{:S(2)}) %all-to-all-start) | async-done | bytes 1654816 | tf_op jit(solution)/shard_map/all_to_all | solution.py:368
  54.5 3.7 %all-to-all-start.3 = ((bf16[16,404,128]{2,1,0:T(8,128)(2,1)}), bf16[16,404,128]{2,1,0:T(8,128)(2,1)S(1)}, u32[]{:S(2)}, u32[]{:S(2)}) async-start(bf16[16,404,128]{2,1,0:T(8,128)(2,1)} %pack_pairs.3), calls=%async_computation.3 | async-start | bytes 3342336 | tf_op jit(solution)/shard_map/all_to_all | solution.py:368
  59.2 16.4 %attend_pair.2 = (bf16[16,192,128]{2,1,0:T(8,128)(2,1)S(1)}, f32[8,128]{1,0:T(8,128)S(1)}) custom-call(s32[1,2]{1,0:T(1,128)S(1)} %copy-done.7, bf16[16,404,128]{2,1,0:T(8,128)(2,1)S(1)} %all-to-all-done.r_ref, bf16[16,64,128]{2,1,0:T(8,128)(2,1)S(1)} %copy-done.9), custom_call_target="tpu_custom_call" | custom-call | flops 4831838208 | bytes 3309568 | tf_op jit(solution)/shard_map/attend_pair/pallas_call | solution.py:225
  76.5 6.1 %all-to-all-done.3.r_ref = bf16[16,404,128]{2,1,0:T(8,128)(2,1)S(1)} async-done(((bf16[16,404,128]{2,1,0:T(8,128)(2,1)}), bf16[16,404,128]{2,1,0:T(8,128)(2,1)S(1)}, u32[]{:S(2)}, u32[]{:S(2)}) %all-to-all-start.3) | async-done | bytes 1654816 | tf_op jit(solution)/shard_map/all_to_all | solution.py:368
  82.6 3.8 %all-to-all-start.2 = ((bf16[16,192,128]{2,1,0:T(8,128)(2,1)}), bf16[16,192,128]{2,1,0:T(8,128)(2,1)S(1)}, u32[]{:S(2)}, u32[]{:S(2)}) async-start(bf16[16,192,128]{2,1,0:T(8,128)(2,1)} %copy-done.1), calls=%async_computation.2 | async-start | bytes 1572864 | tf_op jit(solution)/shard_map/all_to_all | solution.py:368
  86.5 16.5 %attend_pair.3 = (bf16[16,128,128]{2,1,0:T(8,128)(2,1)S(1)}, f32[8,128]{1,0:T(8,128)S(1)}) custom-call(s32[1,2]{1,0:T(1,128)S(1)} %copy-done.7, bf16[16,404,128]{2,1,0:T(8,128)(2,1)S(1)} %all-to-all-done.3.r_ref), custom_call_target="tpu_custom_call" | custom-call | flops 4831838208 | bytes 3309568 | tf_op jit(solution)/shard_map/attend_pair/pallas_call | solution.py:225
  103.7 7.0 %all-to-all-start.4 = ((bf16[16,128,128]{2,1,0:T(8,128)(2,1)}), bf16[16,128,128]{2,1,0:T(8,128)(2,1)S(1)}, u32[]{:S(2)}, u32[]{:S(2)}) async-start(bf16[16,128,128]{2,1,0:T(8,128)(2,1)} %copy-done.2), calls=%async_computation.4 | async-start | bytes 1048576 | tf_op jit(solution)/shard_map/all_to_all | solution.py:368
  112.0 1.6 %collective-permute-start.2 = (f32[128]{0:T(128)S(1)}, f32[128]{0:T(128)S(1)}, u32[]{:S(2)}, u32[]{:S(2)}) collective-permute-start(f32[128]{0:T(128)S(1)} %max.33), channel_id=1, source_target_pairs={{0,16},{16,0},{32,48},{48,32},{1,17},{17,1},{33,49},{49,33},{2,18}... | collective-permute-start | bytes 1544 | tf_op jit(solution)/shard_map/ppermute | solution.py:347
  113.6 1.9 %collective-permute-done.2 = f32[128]{0:T(128)S(1)} collective-permute-done((f32[128]{0:T(128)S(1)}, f32[128]{0:T(128)S(1)}, u32[]{:S(2)}, u32[]{:S(2)}) %collective-permute-start.2) | collective-permute-done | bytes 544 | tf_op jit(solution)/shard_map/ppermute | solution.py:347
  115.5 3.2 %collective-permute-start.3 = (f32[128]{0:T(128)S(1)}, f32[128]{0:T(128)S(1)}, u32[]{:S(2)}, u32[]{:S(2)}) collective-permute-start(f32[128]{0:T(128)S(1)} %max.34), channel_id=1, source_target_pairs={{0,32},{16,48},{32,0},{48,16},{1,33},{17,49},{33,1},{49,17},{2,34}... | collective-permute-start | bytes 1544 | tf_op jit(solution)/shard_map/ppermute | solution.py:347
  118.7 2.8 %all-to-all-done.4.b_ref = bf16[16,128,128]{2,1,0:T(8,128)(2,1)S(1)} async-done(((bf16[16,128,128]{2,1,0:T(8,128)(2,1)}), bf16[16,128,128]{2,1,0:T(8,128)(2,1)S(1)}, u32[]{:S(2)}, u32[]{:S(2)}) %all-to-all-start.4) | async-done | bytes 524320 | tf_op jit(solution)/shard_map/all_to_all | solution.py:368
  121.5 1.3 copy-done
  122.8 11.5 %finish.1 = (f32[2,64,128]{2,1,0:T(8,128)S(1)}, f32[8,128]{1,0:T(8,128)S(1)}) custom-call(f32[2]{0:T(128)S(1)} %copy-done.6, bf16[16,192,128]{2,1,0:T(8,128)(2,1)S(1)} %all-to-all-done.2.a_ref, bf16[16,128,128]{2,1,0:T(8,128)(2,1)S(1)} %all-to-all-done.4.b_ref, bf16[1,2,128,2432]{3,2,1,0:T(8,128)(2,1)S(1)} %copy-done, f32[1,2,2432]{2,1,0:T(2,128)S(1)} %copy-done.5, ...), custom_call_target="tpu_custom_call" | custom-call | flops 3107979264 | bytes 11829248 | tf_op jit(solution)/shard_map/finish/pallas_call | solution.py:322
  135.0 3.0 %collective-permute-done.4 = f32[128]{0:T(128)S(1)} collective-permute-done((f32[128]{0:T(128)S(1)}, f32[128]{0:T(128)S(1)}, u32[]{:S(2)}, u32[]{:S(2)}) %collective-permute-start.4) | collective-permute-done | bytes 544 | tf_op jit(solution)/shard_map/ppermute | solution.py:347
  138.8 4.3 %collective-permute-done.5 = f32[128]{0:T(128)S(1)} collective-permute-done((f32[128]{0:T(128)S(1)}, f32[128]{0:T(128)S(1)}, u32[]{:S(2)}, u32[]{:S(2)}) %collective-permute-start.5) | collective-permute-done | bytes 544 | tf_op jit(solution)/shard_map/ppermute | solution.py:347
  143.0 3.5 %collective-permute-done.6 = f32[128]{0:T(128)S(1)} collective-permute-done((f32[128]{0:T(128)S(1)}, f32[128]{0:T(128)S(1)}, u32[]{:S(2)}, u32[]{:S(2)}) %collective-permute-start.6) | collective-permute-done | bytes 544 | tf_op jit(solution)/shard_map/ppermute | solution.py:347
  147.7 3.9 %collective-permute-done.7 = f32[128]{0:T(128)S(1)} collective-permute-done((f32[128]{0:T(128)S(1)}, f32[128]{0:T(128)S(1)}, u32[]{:S(2)}, u32[]{:S(2)}) %collective-permute-start.7) | collective-permute-done | bytes 544 | tf_op jit(solution)/shard_map/ppermute | solution.py:347
  (56 shorter events, 9.3 us)
Async XLA Ops:
  3.7 23.6 %all-to-all-start.1 = ((bf16[16,212,128]{2,1,0:T(8,128)(2,1)}), bf16[16,212,128]{2,1,0:T(8,128)(2,1)S(1)}, u32[]{:S(2)}, u32[]{:S(2)}) async-start(bf16[16,212,128]{2,1,0:T(8,128)(2,1)} %pack_single.1), calls=%async_computation.1 | async-start | bytes 1769472 | tf_op jit(solution)/shard_map/all_to_all | solution.py:368
  27.3 27.2 %all-to-all-start = ((bf16[16,404,128]{2,1,0:T(8,128)(2,1)}), bf16[16,404,128]{2,1,0:T(8,128)(2,1)S(1)}, u32[]{:S(2)}, u32[]{:S(2)}) async-start(bf16[16,404,128]{2,1,0:T(8,128)(2,1)} %pack_pairs.2), calls=%async_computation | async-start | bytes 3342336 | tf_op jit(solution)/shard_map/all_to_all | solution.py:368
  31.0 3.9 %copy-start.7 = (s32[1,2]{1,0:T(1,128)S(1)}, s32[1,2]{1,0:T(1,128)}, u32[]{:S(2)}) copy-start(s32[1,2]{1,0:T(1,128)} %len_ref.5) | copy-start | bytes 28
  54.5 28.1 %all-to-all-start.3 = ((bf16[16,404,128]{2,1,0:T(8,128)(2,1)}), bf16[16,404,128]{2,1,0:T(8,128)(2,1)S(1)}, u32[]{:S(2)}, u32[]{:S(2)}) async-start(bf16[16,404,128]{2,1,0:T(8,128)(2,1)} %pack_pairs.3), calls=%async_computation.3 | async-start | bytes 3342336 | tf_op jit(solution)/shard_map/all_to_all | solution.py:368
  82.6 21.1 %all-to-all-start.2 = ((bf16[16,192,128]{2,1,0:T(8,128)(2,1)}), bf16[16,192,128]{2,1,0:T(8,128)(2,1)S(1)}, u32[]{:S(2)}, u32[]{:S(2)}) async-start(bf16[16,192,128]{2,1,0:T(8,128)(2,1)} %copy-done.1), calls=%async_computation.2 | async-start | bytes 1572864 | tf_op jit(solution)/shard_map/all_to_all | solution.py:368
  86.4 27.2 %copy-start.11 = (f32[2432]{0:T(1024)S(1)}, f32[2432]{0:T(1024)}, u32[]{:S(2)}) copy-start(f32[2432]{0:T(1024)} %param.27) | copy-start | bytes 29188
  86.4 35.1 %copy-start.3 = (bf16[2432,64]{0,1:T(8,128)(2,1)S(1)}, bf16[2432,64]{0,1:T(8,128)(2,1)}, u32[]{:S(2)}) copy-start(bf16[2432,64]{0,1:T(8,128)(2,1)} %param.30) | copy-start | bytes 933892
  86.4 35.1 %copy-start.4 = (f32[1,2,2,2432]{3,2,1,0:T(2,128)S(1)}, f32[1,2,2,2432]{3,2,1,0:T(2,128)}, u32[]{:S(2)}) copy-start(f32[1,2,2,2432]{3,2,1,0:T(2,128)} %mod_ref.1) | copy-start | bytes 116740
  86.4 35.1 %copy-start.5 = (f32[1,2,2432]{2,1,0:T(2,128)S(1)}, f32[1,2,2432]{2,1,0:T(2,128)}, u32[]{:S(2)}) copy-start(f32[1,2,2432]{2,1,0:T(2,128)} %gate_ref.1) | copy-start | bytes 58372
  86.5 35.0 %copy-start.6 = (f32[2]{0:T(128)S(1)}, f32[2]{0:T(128)}, u32[]{:S(2)}) copy-start(f32[2]{0:T(128)} %guide_ref.1) | copy-start | bytes 28
  103.7 17.8 %all-to-all-start.4 = ((bf16[16,128,128]{2,1,0:T(8,128)(2,1)}), bf16[16,128,128]{2,1,0:T(8,128)(2,1)S(1)}, u32[]{:S(2)}, u32[]{:S(2)}) async-start(bf16[16,128,128]{2,1,0:T(8,128)(2,1)} %copy-done.2), calls=%async_computation.4 | async-start | bytes 1048576 | tf_op jit(solution)/shard_map/all_to_all | solution.py:368
  110.8 1.2 collective-permute-start.1
  112.0 3.5 %collective-permute-start.2 = (f32[128]{0:T(128)S(1)}, f32[128]{0:T(128)S(1)}, u32[]{:S(2)}, u32[]{:S(2)}) collective-permute-start(f32[128]{0:T(128)S(1)} %max.33), channel_id=1, source_target_pairs={{0,16},{16,0},{32,48},{48,32},{1,17},{17,1},{33,49},{49,33},{2,18}... | collective-permute-start | bytes 1544 | tf_op jit(solution)/shard_map/ppermute | solution.py:347
  115.5 18.8 %collective-permute-start.3 = (f32[128]{0:T(128)S(1)}, f32[128]{0:T(128)S(1)}, u32[]{:S(2)}, u32[]{:S(2)}) collective-permute-start(f32[128]{0:T(128)S(1)} %max.34), channel_id=1, source_target_pairs={{0,32},{16,48},{32,0},{48,16},{1,33},{17,49},{33,1},{49,17},{2,34}... | collective-permute-start | bytes 1544 | tf_op jit(solution)/shard_map/ppermute | solution.py:347
  121.5 1.3 copy-start
  122.8 15.9 %copy-start.14 = (s32[2]{0:T(128)S(1)}, s32[2]{0:T(128)}, u32[]{:S(2)}) copy-start(s32[2]{0:T(128)} %param.32) | copy-start | bytes 28
  122.8 24.6 %copy-start.13 = (s32[38]{0:T(128)S(1)}, s32[38]{0:T(128)}, u32[]{:S(2)}) copy-start(s32[38]{0:T(128)} %param.25) | copy-start | bytes 460
  122.8 30.1 %copy-start.10 = (f32[2,128,64]{1,2,0:T(8,128)S(1)}, f32[2,128,64]{1,2,0:T(8,128)}, u32[]{:S(2)}) copy-start(f32[2,128,64]{1,2,0:T(8,128)} %param.17) | copy-start | bytes 196612
  122.8 30.1 %copy-start.12 = (f32[64]{0:T(128)S(1)}, f32[64]{0:T(128)}, u32[]{:S(2)}) copy-start(f32[64]{0:T(128)} %param.31) | copy-start | bytes 772
  134.3 3.6 %collective-permute-start.4 = (f32[128]{0:T(128)S(1)}, f32[128]{0:T(128)S(1)}, u32[]{:S(2)}, u32[]{:S(2)}) collective-permute-start(f32[128]{0:T(128)S(1)} %compare_select_fusion.4), channel_id=1, source_target_pairs={{0,1},{1,0},{2,3},{3,2},{4,5},{5,4},{6,7},{7,6},{8,9},{9,8},{10,11... | collective-permute-start | bytes 1544 | tf_op jit(solution)/shard_map/ppermute | solution.py:347
  138.0 5.0 %collective-permute-start.5 = (f32[128]{0:T(128)S(1)}, f32[128]{0:T(128)S(1)}, u32[]{:S(2)}, u32[]{:S(2)}) collective-permute-start(f32[128]{0:T(128)S(1)} %add_select_fusion.3), channel_id=1, source_target_pairs={{0,2},{1,3},{2,0},{3,1},{4,6},{5,7},{6,4},{7,5},{8,10},{9,11},{10,... | collective-permute-start | bytes 1544 | tf_op jit(solution)/shard_map/ppermute | solution.py:347
  143.0 3.5 %collective-permute-start.6 = (f32[128]{0:T(128)S(1)}, f32[128]{0:T(128)S(1)}, u32[]{:S(2)}, u32[]{:S(2)}) collective-permute-start(f32[128]{0:T(128)S(1)} %add_select_fusion.2), channel_id=1, source_target_pairs={{0,4},{1,5},{2,6},{3,7},{4,0},{5,1},{6,2},{7,3},{8,12},{9,13},{10,... | collective-permute-start | bytes 1544 | tf_op jit(solution)/shard_map/ppermute | solution.py:347
  146.6 5.0 %collective-permute-start.7 = (f32[128]{0:T(128)S(1)}, f32[128]{0:T(128)S(1)}, u32[]{:S(2)}, u32[]{:S(2)}) collective-permute-start(f32[128]{0:T(128)S(1)} %add_select_fusion.1), channel_id=1, source_target_pairs={{0,8},{1,9},{2,10},{3,11},{4,12},{5,13},{6,14},{7,15},{8,0},{9,1},... | collective-permute-start | bytes 1544 | tf_op jit(solution)/shard_map/ppermute | solution.py:347
  147.6 5.3 %collective-permute-start = (f32[2,64,128]{2,1,0:T(8,128)S(1)}, f32[2,64,128]{2,1,0:T(8,128)S(1)}, u32[]{:S(2)}, u32[]{:S(2)}) collective-permute-start(f32[2,64,128]{2,1,0:T(8,128)S(1)} %get-tuple-element.19), channel_id=1, source_target_pairs={{0,64},{64,0},{1,65},{65,1},{2,66},{66,2},{3,67},{67,3},{4,68},{68... | collective-permute-start | bytes 196616 | tf_op jit(solution)/shard_map/ppermute | solution.py:384
  (4 other events, 3.4 us)
